TPU v7x, 32 devices: a whole 2x2x4 slice. The times are simulated.
32 devices in a mesh: groups: 2 (over x), seq: 8 (over z, y), tensor: 2 (over core).
Axes of the slice: x: 2, y: 2, z: 4, core: 2. Of those that a mesh axis runs over, the one named last changes fastest.
Arguments:
- queries: bfloat16 [128, 2, 8192], P(('groups', 'seq'), None, 'tensor'), parts along dimension 0, may hold values from -384 to 384
- fresh_keys: bfloat16 [128, 2, 1024], P(('groups', 'seq'), None, 'tensor'), parts along dimension 0, may hold values from -24 to 24
- fresh_values: bfloat16 [128, 2, 1024], P(('groups', 'seq'), None, 'tensor'), parts along dimension 0, may hold values from -6 to 6
- residual_in: bfloat16 [128, 2, 8192], P(('groups', 'seq'), None, 'tensor'), parts along dimension 0, may hold values from -0.29882812 to 0.29882812
- cache_keys: bfloat16 [8, 8192, 128], P('tensor', ('groups', 'seq')), parts along dimension 1, may hold values from -8 to 8
- cache_values: bfloat16 [8, 8192, 128], P('tensor', ('groups', 'seq')), parts along dimension 1, may hold values from -6 to 6
- key_scales: float32 [8, 128], P('tensor', ('groups', 'seq')), parts along dimension 1, may hold values from 0.5 to 2
- value_scales: float32 [8, 128], P('tensor', ('groups', 'seq')), parts along dimension 1, may hold values from 0.5 to 2
- page_table: int32 [16, 8], P(('groups', 'seq')), parts along dimension 0, may hold values from 0 to 7, each once within a row
- row_lengths: int32 [128], P('groups'), parts along dimension 0, may hold values from 512 to 4096
- norm_gain: float32 [8192], P('tensor'), may hold values from 0.1 to 1.9
- w_gate: bfloat16 [8192, 14336], P('tensor', 'seq'), may hold values from -0.0625 to 0.0625
- w_up: bfloat16 [8192, 14336], P('tensor', 'seq'), may hold values from -0.0625 to 0.0625
- w_down: bfloat16 [14336, 8192], P('seq', 'tensor'), may hold values from -0.046875 to 0.046875
Outputs:
- layer_out: bfloat16 [128, 2, 8192], P(('groups', 'seq'), None, 'tensor'), parts along dimension 0
There are 2 independent parts, one for each index of `groups`. A program takes and returns all parts, laid end to end along the dimension named above; an argument that names none is the same for every part. Nothing has to cross between parts.
Inputs may be any that keep to these rules, and one draw needn't show every extreme that they name: Each row of page_table names each of its seq index's pages once. `row_lengths`: every row sees at least the cache positions of the first seq index.
All inputs are finite; a program needn't handle non-finite values.
Results may differ from a plain program's by a relative error of at most 0.0064.
Values may be sent and summed in bfloat16 or wider, within the bound.
No kernel may reach another device: no remote copies, remote signals or barrier semaphores. Data moves between devices by JAX's collectives and lax.ppermute only.
A program may use at most 128 MiB of HBM per device.

v0:
```python
import math

import jax
import jax.numpy as jnp
from jax import lax
from jax.sharding import PartitionSpec as P

D = 8192


NEG_FILL = -1e30
EPSILON = 1e-05
LOG2E = 1.4426950408889634


def combine_partials(earlier, later):
    shared_top = jnp.maximum(earlier[0], later[0])
    early_factor = jnp.exp2(earlier[0] - shared_top)
    late_factor = jnp.exp2(later[0] - shared_top)
    return (
        shared_top,
        earlier[1] * early_factor + later[1] * late_factor,
        earlier[2] * early_factor[..., None] + later[2] * late_factor[..., None],
    )


def masked_terms(scores, allowed_mask):
    row_top = jnp.ceil(jnp.max(jnp.where(allowed_mask, scores, NEG_FILL), axis=-1))
    exp_terms = jnp.where(allowed_mask, jnp.exp2(scores - row_top[..., None]), 0.0)
    return (row_top, exp_terms)


def body(
    queries,
    fresh_keys,
    fresh_values,
    residual_in,
    cache_keys,
    cache_values,
    key_scales,
    value_scales,
    page_table,
    row_lengths,
    norm_gain,
    w_gate,
    w_up,
    w_down,
):
    local_rows = queries.shape[0]
    step_count = queries.shape[1]
    half_width = queries.shape[2]
    groups = cache_keys.shape[0]
    cache_span = cache_keys.shape[1]
    head_dim = cache_keys.shape[2]
    page_count = page_table.shape[1]
    block_size = cache_span // page_count
    heads_per = half_width // (groups * head_dim)
    inv_root = LOG2E / math.sqrt(head_dim)
    seq_index = lax.axis_index("seq")
    all_q, all_fk, all_fv, all_x = (
        lax.all_gather(queries, "seq", axis=0, tiled=True),
        lax.all_gather(fresh_keys, "seq", axis=0, tiled=True),
        lax.all_gather(fresh_values, "seq", axis=0, tiled=True),
        lax.all_gather(residual_in, "seq", axis=0, tiled=True),
    )
    all_rows = all_q.shape[0]
    offsets = jnp.arange(cache_span, dtype=jnp.int32)
    logical = seq_index * page_count + jnp.repeat(page_table[0], block_size)
    position = logical * block_size + offsets % block_size
    visible = position[None, :] < row_lengths[:, None]
    k_scale = jnp.repeat(key_scales, block_size, axis=1)
    v_scale = jnp.repeat(value_scales, block_size, axis=1)
    q_part = all_q.reshape(all_rows, step_count, groups, heads_per, head_dim)
    q_part = jnp.moveaxis(q_part, 2, 0)

    def per_group(operands):
        q_group, key_block, value_block, k_row, v_row = operands
        raw_scores = jnp.einsum(
            "nsqd,cd->nsqc", q_group, key_block, preferred_element_type=jnp.float32
        )
        scores = raw_scores * k_row * inv_root
        row_top, exp_terms = masked_terms(scores, visible[:, None, None, :])
        row_total = jnp.sum(exp_terms, axis=-1)
        weights = (exp_terms * v_row).astype(jnp.bfloat16)
        weighted = jnp.einsum(
            "nsqc,cd->nsqd", weights, value_block, preferred_element_type=jnp.float32
        )
        return (row_top, row_total, weighted)

    partial_value = lax.map(per_group, (q_part, cache_keys, cache_values, k_scale, v_scale))
    row_peak = lax.pmax(partial_value[0], "seq")
    factor = jnp.exp2(partial_value[0] - row_peak)
    row_total, weighted = lax.psum(
        (partial_value[1] * factor, partial_value[2] * factor[..., None]), "seq"
    )
    row_count = all_q.shape[0]
    fresh_row_count = all_q.shape[0]
    q_part = all_q.reshape(fresh_row_count, step_count, groups, heads_per, head_dim)
    k_part = all_fk.reshape(fresh_row_count, step_count, groups, head_dim)
    v_part = all_fv.reshape(fresh_row_count, step_count, groups, head_dim)
    raw_scores = jnp.einsum("nsgqd,ntgd->gnsqt", q_part, k_part, preferred_element_type=jnp.float32)
    scores = raw_scores * inv_root
    allowed = jnp.arange(step_count)[None, :] <= (0 + jnp.arange(step_count))[:, None]
    row_top, exp_terms = masked_terms(scores, allowed[None, None, :, None, :])
    fresh_row_total = jnp.sum(exp_terms, axis=-1)
    fresh_weighted = jnp.einsum(
        "gnsqt,ntgd->gnsqd",
        exp_terms.astype(jnp.bfloat16),
        v_part,
        preferred_element_type=jnp.float32,
    )
    joined = combine_partials(
        (row_peak, row_total, weighted), (row_top, fresh_row_total, fresh_weighted)
    )
    attention = joined[2] / joined[1][..., None]
    attention = jnp.moveaxis(attention, 0, 2).reshape(row_count, step_count, half_width)
    hidden_state = all_x.astype(jnp.float32) + attention
    square = lax.psum(jnp.sum(hidden_state * hidden_state, axis=-1), "tensor")
    inverse_rms = lax.rsqrt(square / D + EPSILON)
    normed = (hidden_state * inverse_rms[..., None] * norm_gain).astype(jnp.bfloat16)
    hidden_state, normed = (hidden_state, normed)
    own_state = lax.dynamic_slice_in_dim(hidden_state, seq_index * local_rows, local_rows, 0)
    flat_normed = normed.reshape(all_rows * step_count, half_width)
    gate_part = jnp.dot(flat_normed, w_gate, preferred_element_type=jnp.float32)
    up_part = jnp.dot(flat_normed, w_up, preferred_element_type=jnp.float32)
    gate_sums, up_sums = lax.psum((gate_part, up_part), "tensor")
    hidden = (jax.nn.silu(gate_sums) * up_sums).astype(jnp.bfloat16)
    down_sums = lax.psum_scatter(
        jnp.dot(hidden, w_down, preferred_element_type=jnp.float32),
        "seq",
        scatter_dimension=0,
        tiled=True,
    )
    return (own_state + down_sums.reshape(local_rows, step_count, half_width)).astype(jnp.bfloat16)


def solution(mesh):
    in_specs = (
        P(("groups", "seq"), None, "tensor"),
        P(("groups", "seq"), None, "tensor"),
        P(("groups", "seq"), None, "tensor"),
        P(("groups", "seq"), None, "tensor"),
        P("tensor", ("groups", "seq"), None),
        P("tensor", ("groups", "seq"), None),
        P("tensor", ("groups", "seq")),
        P("tensor", ("groups", "seq")),
        P(("groups", "seq"), None),
        P("groups"),
        P("tensor"),
        P("tensor", "seq"),
        P("tensor", "seq"),
        P("seq", "tensor"),
    )
    out_specs = P(("groups", "seq"), None, "tensor")
    return jax.shard_map(body, mesh=mesh, in_specs=in_specs, out_specs=out_specs, check_vma=False)
```

profile of v0, /device:TPU:0, one launch (start us, length us, event | category | flops | bytes accessed | tf_op | source)
XLA Modules:
  0.0 390.4 jit_solution(16728039884289439175)
XLA Ops:
  9.8 42.7 %all-gather.5.cloned.1.call-done = bf16[64,2,4096]{2,1,0:T(2,128)(2,1)} async-done(((bf16[8,2,4096]{2,1,0:T(2,128)(2,1)}), bf16[64,2,4096]{2,1,0:T(2,128)(2,1)}) %all-gather.5.cloned.1.call-update) | async-done | bytes 1048592 | tf_op jit(solution)/shard_map/all_gather | solution.py:61
  52.5 1.9 reshape.100
  54.4 21.1 %while.15 = (s32[]{:T(128)}, f32[4,64,2,8]{1,3,2,0:T(8,128)S(1)}, f32[4,64,2,8]{1,3,2,0:T(8,128)S(1)}, f32[4,64,2,8,128]{4,3,2,1,0:T(8,128)}, bf16[4,64,2,8,128]...) while((s32[]{:T(128)}, f32[4,64,2,8]{1,3,2,0:T(8,128)S(1)}, ...), condition=%wide.region_3.4_spmd.clone, body=%wide.region_0.3_spmd.clone.sunk | while | flops 277380096 | bytes 7569801 | solution.py:90
  54.5 1.6 select_reduce_fusion.3
  57.1 2.5 fusion.57
  59.8 1.6 select_reduce_fusion.3
  61.5 0.9 fusion.56
  62.4 2.5 fusion.57
  65.1 1.6 select_reduce_fusion.3
  67.7 2.5 fusion.57
  70.3 1.6 select_reduce_fusion.3
  73.0 2.5 fusion.57
  75.5 34.9 %pmax.7 = f32[4,64,2,8]{1,3,2,0:T(8,128)S(1)} all-reduce(f32[4,64,2,8]{1,3,2,0:T(8,128)S(1)} %get-tuple-element.60), channel_id=1, replica_groups=mesh['groups'=2,'seq'=8,'tensor'=2] {'seq'}, use_global_device_ids=true, to_apply=%region_4.5 | all-reduce | flops 4096 | bytes 32768 | tf_op jit(solution)/shard_map/pmax | solution.py:91
  110.6 3.6 broadcast_multiply_fusion
  115.8 31.6 %all_gather.14 = bf16[64,2,512]{2,1,0:T(2,128)(2,1)S(1)} all-gather(bf16[8,2,512]{2,1,0:T(2,128)(2,1)S(1)} %copy-done.2), channel_id=1, replica_groups=mesh['groups'=2,'seq'=8,'tensor'=2] {'seq'}, dimensions={0}, use_global_device_ids=true | all-gather | bytes 147456 | tf_op jit(solution)/shard_map/all_gather | solution.py:62
  147.6 30.9 %all_gather.15 = bf16[64,2,512]{2,1,0:T(2,128)(2,1)S(1)} all-gather(bf16[8,2,512]{2,1,0:T(2,128)(2,1)S(1)} %copy-done.3), channel_id=1, replica_groups=mesh['groups'=2,'seq'=8,'tensor'=2] {'seq'}, dimensions={0}, use_global_device_ids=true | all-gather | bytes 147456 | tf_op jit(solution)/shard_map/all_gather | solution.py:63
  178.5 4.8 %select_reduce_fusion.1 = (f32[4,64,2,8]{3,2,1,0:T(2,128)S(1)}, f32[4,64,2,8,2]{3,4,2,1,0:T(2,128)S(1)}) fusion(pred[2,2]{1,0:T(4,128)(4,1)S(1)} %iota_compare_fusion, bf16[64,2,4,128,1]{3,2,1,0,4:T(4,128)(2,1)S(1)} %bitcast.70, bf16[64,2,4,8,128]{4,3,2,1,0:T(8,128)(2,1)S(1)} %bitcast.65), kind=kOutput, calls=%fused_computation.41 | convolution fusion | flops 2117632 | bytes 1228804 | tf_op jit(solution)/shard_map/nsgqd,ntgd->gnsqt/dot_general | solution.py:101
  183.6 1.2 fusion.38
  184.9 34.3 %psum.36 = f32[4,64,2,8]{1,3,2,0:T(8,128)S(1)} all-reduce(f32[4,64,2,8]{1,3,2,0:T(8,128)S(1)} %get-tuple-element.172), channel_id=1, replica_groups=mesh['groups'=2,'seq'=8,'tensor'=2] {'seq'}, use_global_device_ids=true, to_apply=%region_7.8 | all-reduce | flops 4096 | bytes 32768 | tf_op jit(solution)/shard_map/psum | solution.py:93
  219.7 4.1 %divide_bitcast_fusion = f32[64,2,4,8,128]{4,3,1,0,2:T(8,128)S(1)} fusion(f32[4,64,2,8,128]{4,3,2,1,0:T(8,128)} %all-reduce.4.cloned.1.call-done, f32[4,64,2,8]{3,2,1,0:T(2,128)S(1)} %copy.91, f32[4,64,2,8]{3,2,1,0:T(2,128)S(1)} %copy.88, f32[4,64,2,8]{3,2,1,0:T(2,128)S(1)} %copy.84, bf16[64,2,4,128,1]{3,2,1,0,4:T(4,128)(2,1)S(1)} %bitcast.69, ...), kind=kOutput, calls=%fused_computation.34 | convolution fusion | flops 4227072 | bytes 4423684 | tf_op jit(solution)/shard_map/gnsqt,ntgd->gnsqd/dot_general | solution.py:106
  224.1 1.6 reshape.93
  225.7 31.8 %all-gather.3.cloned.1.call-done = bf16[64,2,4096]{2,0,1:T(8,128)(2,1)} async-done(((bf16[8,2,4096]{2,0,1:T(8,128)(2,1)}), bf16[64,2,4096]{2,0,1:T(8,128)(2,1)}) %all-gather.3.cloned.1.call-update) | async-done | bytes 1048592 | tf_op jit(solution)/shard_map/all_gather | solution.py:64
  257.5 2.2 multiply_reduce_fusion
  259.7 2.6 psum.37
  262.7 2.1 copy.93
  264.8 1.5 reshape.94
  266.2 8.2 %fusion.44 = f32[128,1792]{1,0:T(8,128)} fusion(bf16[128,4096]{1,0:T(8,128)(2,1)S(1)} %reshape.94, bf16[4096,1792]{1,0:T(8,128)(2,1)} %param.28), kind=kOutput, calls=%fused_computation.71 | convolution fusion | flops 1879048192 | bytes 16646144 | tf_op jit(solution)/shard_map/dot_general | solution.py:125
  274.4 8.2 %fusion.43 = f32[128,1792]{1,0:T(8,128)} fusion(bf16[128,4096]{1,0:T(8,128)(2,1)S(1)} %reshape.94, bf16[4096,1792]{1,0:T(8,128)(2,1)} %param.27), kind=kOutput, calls=%fused_computation.70 | convolution fusion | flops 1879048192 | bytes 16646144 | tf_op jit(solution)/shard_map/dot_general | solution.py:124
  282.7 19.7 %all-reduce.6.cloned.1.call-done = (f32[128,1792]{1,0:T(8,128)}, f32[128,1792]{1,0:T(8,128)}) async-done(((f32[128,1792]{1,0:T(8,128)}, f32[128,1792]{1,0:T(8,128)}), (f32[128,1792]{1,0:T(8,128)}, f32[128,1792]{1,0:T(8,128)})) %all-reduce.6.cloned.1.call-update) | async-done | bytes 1835024 | tf_op jit(solution)/shard_map/psum | solution.py:126
  302.4 9.2 %fusion.23 = f32[128,4096]{1,0:T(8,128)} fusion(bf16[1792,4096]{1,0:T(8,128)(2,1)} %param.29, f32[128,1792]{1,0:T(8,128)} %get-tuple-element.165, f32[128,1792]{1,0:T(8,128)} %get-tuple-element.166), kind=kOutput, calls=%fused_computation.42 | convolution fusion | flops 1880424448 | bytes 18612224 | tf_op jit(solution)/shard_map/dot_general | solution.py:129
  311.7 70.1 %reduce-scatter.2.cloned.1.call-done = f32[16,4096]{1,0:T(8,128)} async-done(((f32[128,4096]{1,0:T(8,128)}), f32[16,4096]{1,0:T(8,128)}) %reduce-scatter.2.cloned.1.call-update) | async-done | bytes 262160 | tf_op jit(solution)/shard_map/reduce_scatter | solution.py:128
  381.8 1.1 reshape.95
  (82 shorter events, 11.5 us)
Async XLA Ops:
  6.5 47.8 %copy-start.4 = (s32[64]{0:T(128)S(1)}, s32[64]{0:T(128)}, u32[]{:S(2)}) copy-start(s32[64]{0:T(128)} %param.25) | copy-start | bytes 772
  6.5 46.0 %all-gather.5.cloned.1.call-start = ((), (), s32[]{:S(2)}) async-start(), calls=%async_computation.2 | async-start | bytes 1179648 | tf_op jit(solution)/shard_map/all_gather | solution.py:61
  7.3 212.5 %all-reduce.4.cloned.1.call-start = ((), (), s32[]{:S(2)}) async-start(), calls=%async_computation.3 | async-start | bytes 4194304 | tf_op jit(solution)/shard_map/psum | solution.py:93
  114.1 0.9 copy-start
  114.1 1.7 copy-start.2
  114.1 33.5 %copy-start.3 = (bf16[8,2,512]{2,1,0:T(2,128)(2,1)S(1)}, bf16[8,2,512]{2,1,0:T(2,128)(2,1)}, u32[]{:S(2)}) copy-start(bf16[8,2,512]{2,1,0:T(2,128)(2,1)} %param.18) | copy-start | bytes 49156
  114.1 143.4 %all-gather.3.cloned.1.call-start = ((), (), s32[]{:S(2)}) async-start(), calls=%async_computation.1 | async-start | bytes 1179648 | tf_op jit(solution)/shard_map/all_gather | solution.py:64
  115.8 186.7 %all-reduce.6.cloned.1.call-start = ((), (), s32[]{:S(2)}) async-start(), calls=%async_computation.5 | async-start | bytes 3670016 | tf_op jit(solution)/shard_map/psum | solution.py:126
  225.7 36.6 %copy-start.1 = (f32[4096]{0:T(1024)S(1)}, f32[4096]{0:T(1024)}, u32[]{:S(2)}) copy-start(f32[4096]{0:T(1024)} %param.26) | copy-start | bytes 49156
  282.6 99.1 %reduce-scatter.2.cloned.1.call-start = ((), (), s32[]{:S(2)}) async-start(), calls=%async_computation.4 | async-start | bytes 2359296 | tf_op jit(solution)/shard_map/reduce_scatter | solution.py:128
Sparse Core Ops, SparseCore 0:
  9.5 42.9 all-gather.4
  114.3 101.3 all-reduce.3
  217.9 39.6 all-gather.2
  282.8 19.6 all-reduce.5
  311.8 69.9 reduce-scatter.1
where the time goes:
time: 391 us; the launch traced here: 390 us
  waiting for transfers between devices  165 us (42%)
  blocking collectives  134 us (34%)
  matrix products  50.9 us (13%)
  local copies, waits for them, and re-layouts  14.4 us (4%)
  between operations  13.3 us (3%)
  other arithmetic  12.1 us (3%)
    reduce_scatter x1, waiting for transfers between devices, body(): lax.psum_scatter(jnp.dot(hidden, w_down, preferred_element_type=jnp.float...  70.1 us
    all_gather x1, waiting for transfers between devices, body(): lax.all_gather(queries, 'seq', axis=0, tiled=True)  42.7 us
    pmax x1, blocking collectives, body(): row_peak = lax.pmax(partial_value[0], 'seq')  34.9 us
    psum x1, blocking collectives, body(): lax.psum((partial_value[1] * factor, partial_value[2] * factor[..., None]...  34.3 us
    all_gather x1, waiting for transfers between devices, body(): lax.all_gather(residual_in, 'seq', axis=0, tiled=True)  31.8 us
    all_gather x1, blocking collectives, body(): lax.all_gather(fresh_keys, 'seq', axis=0, tiled=True)  31.6 us
    all_gather x1, blocking collectives, body(): lax.all_gather(fresh_values, 'seq', axis=0, tiled=True)  30.9 us
    psum x1, waiting for transfers between devices, body(): gate_sums, up_sums = lax.psum((gate_part, up_part), 'tensor')  19.7 us
  transfers between devices with their start and end apart: 5, of which 4 were waited for; matrix products, arithmetic and copies ran while one was open for 4% of the time, Pallas kernels for 0%

commit v1 on v0

v1 whole, which is shorter than its diff:
```python
import functools
import math

import jax
import jax.numpy as jnp
from jax import lax
from jax.experimental import pallas as pl
from jax.experimental.pallas import tpu as pltpu
from jax.sharding import PartitionSpec as P


NEG_FILL = -1e30
TOP_FLOOR = -1e29
EPSILON = 1e-05
LOG2E = 1.4426950408889634
BF = jnp.bfloat16
F32 = jnp.float32
META = 8


def split3(x):
    hi = lax.reduce_precision(x, 8, 7)
    mid = lax.reduce_precision(x - hi, 8, 7)
    return hi, mid, x - hi - mid


def round_up(x, m):
    return (x + m - 1) // m * m


VMEM = pl.BlockSpec(memory_space=pltpu.VMEM)
SMEM = pl.BlockSpec(memory_space=pltpu.SMEM)
HBM = pl.BlockSpec(memory_space=pltpu.HBM)
NT = (((1,), (1,)), ((), ()))
TN = (((0,), (0,)), ((), ()))


def hbm(x):
    return pltpu.with_memory_space_constraint(x, pltpu.HBM)


def resident(x):
    return pltpu.with_memory_space_constraint(x, pltpu.VMEM)


def params(mib):
    return pltpu.CompilerParams(vmem_limit_bytes=mib << 20)


def pack_kernel(dims, scal, k_scale, v_scale, pages_ref, q_ref, res_ref, fk_ref, fv_ref, k_ref, v_ref, *refs):
    hs, n, span, pages, rows, tl = dims
    outs, crosses, sems = refs[:hs], refs[hs : 2 * hs], refs[2 * hs]
    hd = k_ref.shape[2]
    hp = rows // tl
    copies = []
    for d in range(hs):
        target = scal[n + d]
        for j, ref in enumerate((k_ref, v_ref)):
            copy = pltpu.make_async_copy(ref.at[target], outs[d].at[pl.ds(j * span, span)], sems.at[d, j])
            copy.start()
            copies.append(copy)
    index = scal[n + hs]
    q_at = 2 * span + META * pages
    row = lax.broadcasted_iota(jnp.int32, (META, hd), 0)
    for d in range(hs):
        target = scal[n + d]
        tiles = []
        for page in range(pages):
            page_id = (index * pages + pages_ref[0, page]).astype(F32)
            value = jnp.where(row < 3, k_scale[target, page], jnp.where(row < 6, v_scale[target, page], page_id))
            hi = value.astype(BF).astype(F32)
            mid = (value - hi).astype(BF).astype(F32)
            low = value - hi - mid
            first = (row == 0) | (row == 3) | (row >= 6)
            second = (row == 1) | (row == 4)
            tiles.append(jnp.where(first, hi, jnp.where(second, mid, low)))
        for pair in range(pages // 2):
            at = 2 * span + pair * 2 * META
            both = jnp.concatenate([tiles[2 * pair], tiles[2 * pair + 1]], axis=0)
            outs[d][at : at + 2 * META, :] = both.astype(BF)
        for h in range(hp):
            at = pl.multiple_of(target * (hp * hd) + h * hd, hd)
            q = q_ref[:, :, pl.ds(at, hd)].reshape(tl, hd)
            res = res_ref[:, :, pl.ds(at, hd)].reshape(tl, hd)
            outs[d][q_at + h * tl : q_at + (h + 1) * tl, :] = q
            outs[d][q_at + rows + h * tl : q_at + rows + (h + 1) * tl, :] = res
            crosses[d][h * tl : (h + 1) * tl, :] = q
            crosses[d][rows + h * tl : rows + (h + 1) * tl, :] = res
        at = pl.multiple_of(target * hd, hd)
        f_at = q_at + 2 * rows
        outs[d][f_at : f_at + tl, :] = fk_ref[:, :, pl.ds(at, hd)].reshape(tl, hd)
        outs[d][f_at + tl : f_at + 2 * tl, :] = fv_ref[:, :, pl.ds(at, hd)].reshape(tl, hd)
    for copy in copies:
        copy.wait()


def attention_kernel(dims, scal, row_len, *refs):
    hs, n, span, pages, rows, tl, steps, first_source, count = dims
    blocks = refs[:hs]
    crosses = refs[hs:n]
    acc_ref, stat_ref, send_ref, qs, ks, vs, fk, fv, scale, lens_ref = refs[n:]
    hd = ks.shape[1]
    blk = span // pages
    nq = count * rows
    q_at = 2 * span + META * pages
    inv_root = LOG2E / math.sqrt(hd)
    for d in range(n):
        ref, at = (blocks[d], q_at) if d < hs else (crosses[d - hs], 0)
        start = pl.multiple_of(scal[d] * rows, rows)
        qs[pl.ds(start, rows), :] = ref[at : at + rows, :]
    f_at = q_at + 2 * rows
    fresh = fk.shape[0] // hs
    for d in range(hs):
        ks[d * span : (d + 1) * span, :] = blocks[d][0:span, :]
        vs[d * span : (d + 1) * span, :] = blocks[d][span : 2 * span, :]
        fk[d * fresh : (d + 1) * fresh, :] = blocks[d][f_at : f_at + fresh, :]
        fv[d * fresh : (d + 1) * fresh, :] = blocks[d][f_at + fresh : f_at + 2 * fresh, :]
        meta = blocks[d][2 * span : 2 * span + META * pages, :].astype(F32)
        for page in range(pages):
            m = meta[page * META : (page + 1) * META, :]
            k_row = (m[0:1] + m[1:2] + m[2:3]) * inv_root
            v_row = m[3:4] + m[4:5] + m[5:6]
            at = (d * pages + page) * META
            scale[at : at + META, :] = jnp.concatenate([k_row, v_row, m[6:7] * float(blk), m[3:8]], axis=0)
    lanes = min(256, nq)
    base_q = first_source * rows
    lane = lax.broadcasted_iota(jnp.int32, (1, nq), 1)
    rl = tl // steps
    lane_row = (lane // rows) * rl + (lane % tl) // steps
    lens = jnp.zeros((1, nq), F32)
    for j in range(count * rl):
        lens = jnp.where(lane_row == j, row_len[first_source * rl + j].astype(F32), lens)
    lens_ref[...] = lens

    def chunk(c, carry):
        at = pl.multiple_of(c * lanes, lanes)
        at_q = pl.multiple_of(base_q + c * lanes, lanes)
        q = qs[pl.ds(at_q, lanes), :]
        length = lens_ref[0:1, pl.ds(at, lanes)]
        raw = lax.dot_general(ks[...], q, NT, preferred_element_type=F32)
        inner = lax.broadcasted_iota(jnp.int32, (blk, lanes), 0).astype(F32)
        scores = []
        for page in range(hs * pages):
            k_scale = scale[page * META : page * META + 1, 0:1]
            limit = length - scale[page * META + 2 : page * META + 3, 0:1]
            part = raw[page * blk : (page + 1) * blk, :] * k_scale
            scores.append(jnp.where(inner < limit, part, NEG_FILL))
        lane = lax.broadcasted_iota(jnp.int32, (1, lanes), 1) + at_q
        source = lane // rows
        token = lane % tl
        fi = lax.broadcasted_iota(jnp.int32, (fk.shape[0], 1), 0)
        f_slot = fi // fresh
        f_token = fi % fresh
        f_source = jnp.where(f_token < tl, scal[0], -1)
        for d in range(1, hs):
            f_source = jnp.where((f_slot == d) & (f_token < tl), scal[d], f_source)
        keep = (f_source == source) & (f_token // steps == token // steps) & (f_token % steps <= token % steps)
        raw_f = lax.dot_general(fk[...], q, NT, preferred_element_type=F32) * inv_root
        fresh_scores = jnp.where(keep, raw_f, NEG_FILL)
        top = jnp.max(fresh_scores, axis=0, keepdims=True)
        for part in scores:
            top = jnp.maximum(top, jnp.max(part, axis=0, keepdims=True))
        top = jnp.maximum(jnp.ceil(top), TOP_FLOOR)
        fresh_terms = jnp.exp2(fresh_scores - top)
        total = jnp.sum(fresh_terms, axis=0, keepdims=True)
        weights = []
        for page, part in enumerate(scores):
            terms = jnp.exp2(part - top)
            total = total + jnp.sum(terms, axis=0, keepdims=True)
            weights.append((terms * scale[page * META + 1 : page * META + 2, 0:1]).astype(BF))
        weight = jnp.concatenate(weights, axis=0)
        acc = lax.dot_general(vs[...], weight, TN, preferred_element_type=F32)
        acc = acc + lax.dot_general(fv[...], fresh_terms.astype(BF), TN, preferred_element_type=F32)
        acc_ref[:, pl.ds(at, lanes)] = acc
        send_ref[0:hd, pl.ds(at, lanes)] = acc.astype(BF)
        zero = jnp.zeros((1, lanes), F32)
        stat_ref[:, pl.ds(at, lanes)] = jnp.concatenate([top, total] + [zero] * 6, axis=0)
        pieces = []
        for value in (top, total):
            hi = value.astype(BF).astype(F32)
            mid = (value - hi).astype(BF).astype(F32)
            pieces += [hi, mid, value - hi - mid]
        pieces += [zero] * 10
        send_ref[hd : hd + 16, pl.ds(at, lanes)] = jnp.concatenate(pieces, axis=0).astype(BF)
        return carry

    lax.fori_loop(0, nq // lanes, chunk, 0)


def combine_kernel(dims, scal, acc_ref, stat_ref, gain_ref, *refs):
    hs, r, rows, tl, aligned, res_at, first_source, count = dims
    n = hs * r
    received = refs[: r - 1]
    blocks = refs[r - 1 : r - 1 + hs]
    crosses = refs[r - 1 + hs : r - 1 + n]
    out_ref, res = refs[r - 1 + n :]
    hd = acc_ref.shape[0]
    hp = rows // tl
    per = count // hs
    for d in range(n):
        ref, at = (blocks[d], res_at) if d < hs else (crosses[d - hs], rows)
        start = pl.multiple_of(scal[d] * rows, rows)
        res[pl.ds(start, rows), :] = ref[at : at + rows, :]
    top = stat_ref[0:1, :]
    total = stat_ref[1:2, :]
    others = []
    for ref in received:
        stats = ref[hd : hd + 16, :].astype(F32)
        o_top = stats[0:1, :] + stats[1:2, :] + stats[2:3, :]
        o_total = stats[3:4, :] + stats[4:5, :] + stats[5:6, :]
        others.append((o_top, o_total, ref))
    best = top
    for o_top, _, _ in others:
        best = jnp.maximum(best, o_top)
    factor = jnp.exp2(top - best)
    total = total * factor
    for o_top, o_total, _ in others:
        total = total + o_total * jnp.exp2(o_top - best)
    value = acc_ref[...] * (factor / total)
    for o_top, _, ref in others:
        value = value + ref[0:hd, :].astype(F32) * (jnp.exp2(o_top - best) / total)
    width = hp * hd
    gain = gain_ref[0:1, pl.ds(pl.multiple_of(lax.rem(scal[0], hs) * width, width), width)]
    for s in range(count):
        part = value[:, s * rows : (s + 1) * rows].T
        at = (first_source + s) * rows
        part = part + res[at : at + rows, :].astype(F32)
        slot = (s % hs) * per + s // hs
        heads = [part[h * tl : (h + 1) * tl, :] * gain[:, h * hd : (h + 1) * hd] for h in range(hp)]
        if aligned:
            for h in range(hp):
                out_ref[slot * tl : (slot + 1) * tl, h * hd : (h + 1) * hd] = heads[h].astype(BF)
        else:
            out_ref[slot] = jnp.concatenate(heads, axis=0).astype(BF)


def prefetch_kernel(count, pieces, *refs):
    ins, outs, sems = refs[:count], refs[count : 2 * count], refs[2 * count]
    copies = []
    for j in range(count):
        step = ins[j].shape[0] // pieces
        for c in range(pieces):
            at = pl.ds(c * step, step)
            copy = pltpu.make_async_copy(ins[j].at[at], outs[j].at[at], sems.at[j, c])
            copy.start()
            copies.append(copy)
    for copy in copies:
        copy.wait()


def prefetch(*arrays):
    count = len(arrays)
    pieces = 4
    return pl.pallas_call(
        functools.partial(prefetch_kernel, count, pieces),
        out_shape=[pltpu.VMEM(x.shape, x.dtype) for x in arrays],
        in_specs=[HBM] * count,
        out_specs=[VMEM] * count,
        scratch_shapes=[pltpu.SemaphoreType.DMA((count, pieces))],
        compiler_params=params(1),
    )(*[hbm(x) for x in arrays])


def gate_up_kernel(dims, scal, *refs):
    first, offsets, halves, ffl, tile = dims
    if first:
        state = ()
    else:
        state, refs = refs[:2], refs[2:]
    parts = refs[: len(offsets) * halves]
    gain_ref, wg_ref, wu_ref = refs[len(parts) : len(parts) + 3]
    outs = refs[len(parts) + 3 :]
    p_all = outs[-1]
    out_ref, ssq_ref = outs[0], outs[1]
    per, width = parts[0].shape
    hs = wg_ref.shape[0] // width
    ffp = out_ref.shape[1] // 2
    starts = [pl.multiple_of(lax.rem(scal[d], hs) * width, width) for d in offsets]
    for k in range(len(offsets)):
        for j in range(halves):
            p_all[k, j * per : (j + 1) * per, :] = parts[k * halves + j][...]

    def column(at, size):
        for base, w_ref in ((0, wg_ref), (ffp, wu_ref)):
            value = None if first else state[0][:, pl.ds(base + at, size)]
            for k, start in enumerate(starts):
                term = jnp.dot(
                    p_all[k], w_ref[pl.ds(start, width), pl.ds(at, size)], preferred_element_type=F32
                )
                value = term if value is None else value + term
            out_ref[:, pl.ds(base + at, size)] = value
            if not first:
                outs[2][:, pl.ds(base + at, size)] = value.astype(BF)

    if tile == ffl:
        column(0, ffl)
    else:

        def step(i, carry):
            column(pl.multiple_of(i * tile, tile), tile)
            return carry

        lax.fori_loop(0, ffl // tile, step, 0)
    lanes = ssq_ref.shape[1]
    ssq = jnp.zeros(ssq_ref.shape, F32) if first else state[1][...]
    for k, start in enumerate(starts):
        inverse = 1.0 / gain_ref[0:1, pl.ds(start, width)]
        for c in range(width // lanes):
            cols = slice(c * lanes, (c + 1) * lanes)
            h = p_all[k, :, cols].astype(F32) * inverse[:, cols]
            ssq = ssq + h * h
    if first:
        ssq_ref[...] = ssq
    else:
        total = jnp.sum(ssq, axis=1, keepdims=True) + jnp.zeros(ssq_ref.shape, F32)
        ssq_ref[...] = total
        hi = total.astype(BF).astype(F32)
        mid = (total - hi).astype(BF).astype(F32)
        lane = lax.broadcasted_iota(jnp.int32, total.shape, 1)
        stat = jnp.where(lane == 0, hi, jnp.where(lane == 1, mid, total - hi - mid))
        outs[2][:, 2 * ffp : 2 * ffp + lanes] = stat.astype(BF)


def gate_up(offsets, scal, carry, parts, gain, w_gate, w_up, ffp):
    halves = len(parts) // len(offsets)
    per, width = parts[0].shape
    tokens = per * halves
    ffl = w_gate.shape[1]
    first = carry is None
    tile = 256 if ffl % 256 == 0 else ffl
    out_shape = [
        jax.ShapeDtypeStruct((tokens, 2 * ffp), F32),
        jax.ShapeDtypeStruct((tokens, 128), F32),
    ]
    if not first:
        out_shape.append(jax.ShapeDtypeStruct((tokens, 2 * ffp + 128), BF))
    args = [] if first else list(carry)
    args += list(parts) + [gain, resident(w_gate), resident(w_up)]
    return pl.pallas_call(
        functools.partial(gate_up_kernel, (first, offsets, halves, ffl, tile)),
        out_shape=out_shape,
        in_specs=[SMEM] + [VMEM] * len(args),
        out_specs=[VMEM] * len(out_shape),
        scratch_shapes=[pltpu.VMEM((len(offsets), tokens, width), BF)],
        compiler_params=params(4),
    )(scal, *args)


def down_kernel(dims, scal, *refs):
    first, n, hs, groups, ffl, offset, width, model = dims
    if first:
        own, ssq_ref, other, wd_ref = refs[:4]
        hidden, outs = refs[4], refs[5:]
        ffp = own.shape[1] // 2
        stat = other[:, 2 * ffp : 2 * ffp + 128].astype(F32)
        square = ssq_ref[:, 0:1] + (stat[:, 0:1] + stat[:, 1:2] + stat[:, 2:3])
        inverse = lax.rsqrt(square / model + EPSILON)
        gate = (own[:, 0:ffl] + other[:, 0:ffl].astype(F32)) * inverse
        up = (own[:, ffp : ffp + ffl] + other[:, ffp : ffp + ffl].astype(F32)) * inverse
        hidden[...] = (gate / (1.0 + jnp.exp(-gate)) * up).astype(BF)
    else:
        hidden, wd_ref, outs = refs[0], refs[1], refs[2:]
    pieces, scratch = outs[:-1], outs[-1]
    tokens = hidden.shape[0]
    block = tokens // (hs * groups)
    tile = scratch.shape[1]
    for c in range(width // tile):
        scratch[...] = jnp.dot(
            hidden[...], wd_ref[:, offset + c * tile : offset + (c + 1) * tile], preferred_element_type=F32
        )
        for d in range(hs):
            for g in range(groups):
                at = pl.multiple_of(g * (tokens // groups) + scal[n + d] * block, block)
                pieces[d][g * block : (g + 1) * block, c * tile : (c + 1) * tile] = scratch[
                    pl.ds(at, block), :
                ].astype(pieces[d].dtype)


def down(first, n, hs, groups, scal, args, w_down, offset, width, model):
    tokens = args[0].shape[0]
    ffl = w_down.shape[0]
    per = tokens // hs
    tile = min(width, 512)
    out_shape = [jax.ShapeDtypeStruct((tokens, ffl), BF)] if first else []
    out_shape += [jax.ShapeDtypeStruct((per, width), F32 if d == 0 else BF) for d in range(hs)]
    return pl.pallas_call(
        functools.partial(down_kernel, (first, n, hs, groups, ffl, offset, width, model)),
        out_shape=out_shape,
        in_specs=[SMEM] + [VMEM] * (len(args) + 1),
        out_specs=[VMEM] * len(out_shape),
        scratch_shapes=[pltpu.VMEM((tokens, tile), F32)],
        compiler_params=params(4),
    )(scal, *args, resident(w_down))


def own_kernel(dims, scal, gain_ref, *refs):
    n, hs, groups, tl = dims
    parts, out_ref = refs[:-1], refs[-1]
    per, width = parts[0].shape
    index = scal[n + hs]
    a = lax.rem(index, hs)
    b = index // hs
    rc = n // hs // groups
    slot = (b // rc) * (per // tl) + a * rc + lax.rem(b, rc)
    for d in range(hs):
        h = jnp.zeros((tl, width), F32)
        for g in range(groups):
            part = parts[d * groups + g][...].astype(F32)
            for j in range(per // tl):
                take = slot == g * (per // tl) + j
                h = jnp.where(take, part[j * tl : (j + 1) * tl, :], h)
        start = pl.multiple_of(lax.rem(scal[d], hs) * width, width)
        out_ref[:, pl.ds(start, width)] = h / gain_ref[0:1, pl.ds(start, width)]


def own_state(scal, gain, parts, n, hs, groups, tl):
    half = gain.shape[1]
    return pl.pallas_call(
        functools.partial(own_kernel, (n, hs, groups, tl)),
        out_shape=jax.ShapeDtypeStruct((tl, half), F32),
        in_specs=[SMEM] + [VMEM] * (1 + len(parts)),
        out_specs=VMEM,
        compiler_params=params(8),
    )(scal, gain, *parts)


def square_sum_kernel(dims, scal, *refs):
    n, hs, r, tl = dims
    pieces, mine, aways = refs[:hs], refs[hs], refs[hs + 1 :]
    b = scal[n + hs] // hs
    total = pieces[0][...]
    for ref in pieces[1:]:
        total = total + ref[...].astype(F32)
    rows = [total[j * tl : (j + 1) * tl, :] for j in range(r)]
    for db in range(r):
        want = lax.rem(b + db, r)
        value = rows[0]
        for j in range(1, r):
            value = jnp.where(want == j, rows[j], value)
        if db == 0:
            mine[...] = value
        else:
            aways[db - 1][...] = value.astype(BF)


def square_sum(scal, pieces, n, hs, r, tl):
    width = pieces[0].shape[1]
    return pl.pallas_call(
        functools.partial(square_sum_kernel, (n, hs, r, tl)),
        out_shape=[jax.ShapeDtypeStruct((tl, width), F32)]
        + [jax.ShapeDtypeStruct((tl, width), BF)] * (r - 1),
        in_specs=[SMEM] + [VMEM] * hs,
        out_specs=[VMEM] * r,
        compiler_params=params(8),
    )(scal, *pieces)


def make_body(n):
    def body(
        queries,
        fresh_keys,
        fresh_values,
        residual_in,
        cache_keys,
        cache_values,
        key_scales,
        value_scales,
        page_table,
        row_lengths,
        norm_gain,
        w_gate,
        w_up,
        w_down,
    ):
        rl, steps, half = queries.shape
        kv_heads, span, hd = cache_keys.shape
        pages = page_table.shape[1]
        hp = half // (kv_heads * hd)
        hs = math.gcd(kv_heads, n)
        assert hs == kv_heads and n * pages <= 256
        r = n // hs
        tl = rl * steps
        rows = hp * tl
        nq = n * rows
        width = hp * hd
        ffl = w_gate.shape[1]
        ffp = round_up(ffl, 128)
        model = half * 2
        groups = 2 if r % 2 == 0 else 1
        count = n // groups
        aligned = tl % 16 == 0
        fpad = round_up(tl, 16)
        index = lax.axis_index("seq")
        a = lax.rem(index, hs)
        b = index // hs
        pow2 = hs & (hs - 1) == 0

        def mate(x, d):
            return x ^ d if pow2 else (x + d) % hs

        def origin(x, d):
            return x ^ d if pow2 else (x - d + hs) % hs

        def shift(x, db, da):
            pairs = []
            for i in range(n):
                bi, ai = divmod(i, hs)
                pairs.append((i, ((bi + db) % r) * hs + mate(ai, da)))
            return lax.ppermute(x, "seq", pairs)

        k = jnp.arange(n + hs + 1, dtype=jnp.int32)
        k_source = ((b - k // hs + r) % r) * hs + origin(a, k % hs)
        scal = jnp.where(k < n, k_source, jnp.where(k < n + hs, mate(a, (k - n) % hs), index)).astype(jnp.int32)
        pick = lambda x, i: lax.dynamic_index_in_dim(x, i, 0, keepdims=False)

        length = 2 * span + META * pages + 2 * rows + 2 * fpad
        if aligned:
            packed = pl.pallas_call(
                functools.partial(pack_kernel, (hs, n, span, pages, rows, tl)),
                out_shape=[jax.ShapeDtypeStruct((length, hd), BF)] * hs
                + [jax.ShapeDtypeStruct((2 * rows, hd), BF)] * hs,
                in_specs=[SMEM] * 4 + [VMEM] * 4 + [HBM] * 2,
                out_specs=[VMEM] * (2 * hs),
                scratch_shapes=[pltpu.SemaphoreType.DMA((hs, 2))],
                compiler_params=params(8),
            )(
                scal,
                *[
                    hbm(x)
                    for x in (
                        key_scales,
                        value_scales,
                        page_table,
                        queries,
                        residual_in,
                        fresh_keys,
                        fresh_values,
                        cache_keys,
                        cache_values,
                    )
                ],
            )
            payloads, cross_out = packed[:hs], packed[hs:]
        else:
            page_id = (index * pages + page_table[0]).astype(F32)
            page_id = jnp.broadcast_to(page_id[None, :], (kv_heads, pages))
            zero = jnp.zeros((kv_heads, pages), F32)
            meta = jnp.stack([*split3(key_scales), *split3(value_scales), page_id, zero], axis=-1)
            meta = jnp.broadcast_to(
                meta.reshape(kv_heads, pages * META, 1), (kv_heads, pages * META, hd)
            )
            by_head = lambda x: jnp.moveaxis(x.reshape(tl, kv_heads, -1, hd), 0, 2).reshape(kv_heads, -1, hd)
            pad = ((0, 0), (0, fpad - tl), (0, 0))
            both = jnp.concatenate([by_head(queries), by_head(residual_in)], axis=1)
            payload = jnp.concatenate(
                [
                    cache_keys,
                    cache_values,
                    meta.astype(BF),
                    both,
                    jnp.pad(by_head(fresh_keys), pad),
                    jnp.pad(by_head(fresh_values), pad),
                ],
                axis=1,
            )
            targets = [mate(a, d) for d in range(hs)]
            payloads = [pick(payload, t) for t in targets]
            cross_out = [pick(both, t) for t in targets]
        blocks = [payloads[0]] + [shift(payloads[d], 0, d) for d in range(1, hs)]
        crosses = [shift(cross_out[d], db, d) for db in range(1, r) for d in range(hs)]
        wg, wu = prefetch(w_gate, w_up)
        gain2 = norm_gain.reshape(1, half)
        res_at = 2 * span + META * pages + rows
        nc = count * rows
        partial = []
        for g in range(groups):
            attend = pl.pallas_call(
                functools.partial(
                    attention_kernel, (hs, n, span, pages, rows, tl, steps, g * count, count)
                ),
                out_shape=(
                    jax.ShapeDtypeStruct((hd, nc), F32),
                    jax.ShapeDtypeStruct((8, nc), F32),
                    jax.ShapeDtypeStruct((hd + 16, nc), BF),
                ),
                in_specs=[SMEM, SMEM] + [VMEM] * n,
                out_specs=(VMEM, VMEM, VMEM),
                scratch_shapes=[
                    pltpu.VMEM((nq, hd), BF),
                    pltpu.VMEM((hs * span, hd), BF),
                    pltpu.VMEM((hs * span, hd), BF),
                    pltpu.VMEM((hs * fpad, hd), BF),
                    pltpu.VMEM((hs * fpad, hd), BF),
                    pltpu.VMEM((hs * pages * META, hd), F32),
                    pltpu.VMEM((1, nc), F32),
                ],
                compiler_params=params(8 if aligned else 16),
            )
            acc, stat, sent = attend(scal, hbm(row_lengths), *blocks, *crosses)
            partial.append((acc, stat, [shift(sent, db, 0) for db in range(1, r)]))
        per = count * tl
        mine = []
        for g, (acc, stat, received) in enumerate(partial):
            p_shape = (per, width) if aligned else (count, rows, hd)
            combine = pl.pallas_call(
                functools.partial(combine_kernel, (hs, r, rows, tl, aligned, res_at, g * count, count)),
                out_shape=jax.ShapeDtypeStruct(p_shape, BF),
                in_specs=[SMEM] + [VMEM] * (3 + r - 1 + n),
                out_specs=VMEM,
                scratch_shapes=[pltpu.VMEM((nq, hd), BF)],
                compiler_params=params(6 if aligned else 32),
            )
            p = combine(scal, acc, stat, gain2, *received, *blocks, *crosses)
            if not aligned:
                p = jnp.moveaxis(p.reshape(count, hp, tl, hd), 1, 2).reshape(per, width)
            mine.append(p)
        gathered = [[shift(p, 0, d) for p in mine] for d in range(1, hs)]
        (wd,) = prefetch(w_down)
        carry = gate_up((0,), scal, None, mine, gain2, wg, wu, ffp)
        flat = [p for group in gathered for p in group]
        own, ssq, message = gate_up(tuple(range(1, hs)), scal, carry, flat, gain2, wg, wu, ffp)
        other = lax.ppermute(message, "tensor", [(0, 1), (1, 0)])

        state = own_state(scal, gain2, mine + flat, n, hs, groups, tl)
        chunks = 2
        cw = half // chunks
        sums = []
        args = [own, ssq, other]
        for c in range(chunks):
            pieces = down(c == 0, n, hs, groups, scal, args, wd, c * cw, cw, model)
            if c == 0:
                args, pieces = [pieces[0]], pieces[1:]
            sums.append((pieces[0], [shift(pieces[d], 0, d) for d in range(1, hs)]))
        outs = []
        for c, (total, got) in enumerate(sums):
            result, *aways = square_sum(scal, [total] + got, n, hs, r, tl)
            result = state[:, c * cw : (c + 1) * cw] + result
            for db in range(1, r):
                result = result + shift(aways[db - 1], db, 0).astype(F32)
            outs.append(result.astype(BF))
        return jnp.concatenate(outs, axis=1).reshape(rl, steps, half)

    return body


def solution(mesh):
    in_specs = (
        P(("groups", "seq"), None, "tensor"),
        P(("groups", "seq"), None, "tensor"),
        P(("groups", "seq"), None, "tensor"),
        P(("groups", "seq"), None, "tensor"),
        P("tensor", ("groups", "seq"), None),
        P("tensor", ("groups", "seq"), None),
        P("tensor", ("groups", "seq")),
        P("tensor", ("groups", "seq")),
        P(("groups", "seq"), None),
        P("groups"),
        P("tensor"),
        P("tensor", "seq"),
        P("tensor", "seq"),
        P("seq", "tensor"),
    )
    out_specs = P(("groups", "seq"), None, "tensor")
    body = make_body(mesh.shape["seq"])
    return jax.shard_map(body, mesh=mesh, in_specs=in_specs, out_specs=out_specs, check_vma=False)
```

time: 391 us -> 111 us (0.28)
  blocking collectives: 134 us -> 0 us
  waiting for transfers between devices: 165 us -> 41.5 us
  matrix products: 50.9 us -> 0 us
  Pallas kernels: 0 us -> 39.6 us
  starting transfers between devices: 0.17 us -> 28.1 us
  between operations: 13.3 us -> 0.23 us
  local copies, waits for them, and re-layouts: 14.4 us -> 1.48 us
  other arithmetic: 12.1 us -> 0.07 us
    all_gather x2 -> x0, waiting for transfers between devices: 74.5 us -> none  [the longest x1 42.7 us: body(): lax.all_gather(queries, 'seq', axis=0, tiled=True)]
    reduce_scatter x1 -> x0, waiting for transfers between devices: 70.1 us -> none  [body(): lax.psum_scatter(jnp.dot(hidden, w_down, preferred_element_type=jnp.float...]
    all_gather x2 -> x0, blocking collectives: 62.5 us -> none  [the longest x1 31.6 us: body(): lax.all_gather(fresh_keys, 'seq', axis=0, tiled=True)]
    dot_general x13 -> x0, matrix products: 50.9 us -> none  [the longest x4 10.1 us: per_group(): jnp.einsum('nsqc,cd->nsqd', weights, value_block, preferred_element_type=...]
    ppermute x0 -> x24, waiting for transfers between devices: none -> 41.5 us  [the longest x23 41.5 us: shift(): return lax.ppermute(x, 'seq', pairs)]
    pallas_call x0 -> x14, Pallas kernels: none -> 39.6 us  [the longest x2 14.8 us: prefetch(): pl.pallas_call(functools.partial(prefetch_kernel, count, pieces), out_sha...]
    psum x2 -> x0, blocking collectives: 36.9 us -> none  [the longest x1 34.3 us: body(): lax.psum((partial_value[1] * factor, partial_value[2] * factor[..., None]...]
    pmax x1 -> x0, blocking collectives: 34.9 us -> none  [body(): row_peak = lax.pmax(partial_value[0], 'seq')]
  transfers between devices with their start and end apart: 5 -> 24, of which waited for: 4 -> 12; matrix products, arithmetic and copies ran while one was open for 4% -> 0% of each run, Pallas kernels for 0% -> 22%
where the time goes in v1:
time: 111 us
  waiting for transfers between devices  41.5 us (37%)
  Pallas kernels  39.6 us (36%)
  starting transfers between devices  28.1 us (25%)
  local copies, waits for them, and re-layouts  1.48 us (1%)
    ppermute x23, waiting for transfers between devices, shift(): return lax.ppermute(x, 'seq', pairs)  41.5 us
    ppermute x23, starting transfers between devices, shift(): return lax.ppermute(x, 'seq', pairs)  28 us
    pallas_call x2, Pallas kernels, prefetch(): pl.pallas_call(functools.partial(prefetch_kernel, count, pieces), out_sha...  14.8 us
    pallas_call x2, Pallas kernels, gate_up(): pl.pallas_call(functools.partial(gate_up_kernel, (first, offsets, halves,...  8.11 us
    pallas_call x2, Pallas kernels, body(): acc, stat, sent = attend(scal, hbm(row_lengths), *blocks, *crosses)  7.25 us
    pallas_call x2, Pallas kernels, down(): pl.pallas_call(functools.partial(down_kernel, (first, n, hs, groups, ffl,...  3.79 us
    pallas_call x1, Pallas kernels, body(): pl.pallas_call(functools.partial(pack_kernel, (hs, n, span, pages, rows,...  2.35 us
  transfers between devices with their start and end apart: 24, of which 12 were waited for; matrix products, arithmetic and copies ran while one was open for 0% of the time, Pallas kernels for 22%

profile of v1, /device:TPU:0, one launch (start us, length us, event | category | flops | bytes accessed | tf_op | source)
XLA Modules:
  0.0 111.0 jit_solution(18129351353863887307)
XLA Ops:
  0.0 2.3 %shard_map.136 = (bf16[1376,128]{1,0:T(8,128)(2,1)S(1)}, bf16[1376,128]{1,0:T(8,128)(2,1)S(1)}, bf16[1376,128]{1,0:T(8,128)(2,1)S(1)}, bf16[1376,128]{1,0:T(8,12...) custom-call(s32[13]{0:T(128)S(1)} %compare_select_fusion.5.scal, ...), custom_call_target="tpu_custom_call" | custom-call | tf_op jit(solution)/shard_map/pallas_call | solution.py:518
  2.4 3.1 %collective-permute-start = (bf16[1376,128]{1,0:T(8,128)(2,1)S(1)}, bf16[1376,128]{1,0:T(8,128)(2,1)S(1)}, u32[]{:S(2)}, u32[]{:S(2)}) collective-permute-start(bf16[1376,128]{1,0:T(8,128)(2,1)S(1)} %get-tuple-element.40), channel_id=1, source_target_pairs={{0,2},{2,0},{4,6},{6,4},{8,10},{10,8},{12,14},{14,12},{1,3},{3,1},... | collective-permute-start | bytes 1056776 | tf_op jit(solution)/shard_map/ppermute | solution.py:509
  5.4 1.6 %collective-permute-start.1 = (bf16[1376,128]{1,0:T(8,128)(2,1)S(1)}, bf16[1376,128]{1,0:T(8,128)(2,1)S(1)}, u32[]{:S(2)}, u32[]{:S(2)}) collective-permute-start(bf16[1376,128]{1,0:T(8,128)(2,1)S(1)} %get-tuple-element.41), channel_id=1, source_target_pairs={{0,4},{2,6},{4,0},{6,2},{8,12},{10,14},{12,8},{14,10},{1,5},{3,7},... | collective-permute-start | bytes 1056776 | tf_op jit(solution)/shard_map/ppermute | solution.py:509
  7.0 3.0 %collective-permute-start.3 = (bf16[256,128]{1,0:T(8,128)(2,1)S(1)}, bf16[256,128]{1,0:T(8,128)(2,1)S(1)}, u32[]{:S(2)}, u32[]{:S(2)}) collective-permute-start(bf16[256,128]{1,0:T(8,128)(2,1)S(1)} %get-tuple-element.43), channel_id=1, source_target_pairs={{0,8},{2,10},{4,12},{6,14},{8,0},{10,2},{12,4},{14,6},{1,9},{3,11}... | collective-permute-start | bytes 196616 | tf_op jit(solution)/shard_map/ppermute | solution.py:509
  10.0 1.3 %collective-permute-start.4 = (bf16[256,128]{1,0:T(8,128)(2,1)S(1)}, bf16[256,128]{1,0:T(8,128)(2,1)S(1)}, u32[]{:S(2)}, u32[]{:S(2)}) collective-permute-start(bf16[256,128]{1,0:T(8,128)(2,1)S(1)} %get-tuple-element.44), channel_id=1, source_target_pairs={{0,10},{2,8},{4,14},{6,12},{8,2},{10,0},{12,6},{14,4},{1,11},{3,9}... | collective-permute-start | bytes 196616 | tf_op jit(solution)/shard_map/ppermute | solution.py:509
  11.3 12.6 %collective-permute-done.3.refs_4_.refs_5_ = bf16[256,128]{1,0:T(8,128)(2,1)S(1)} collective-permute-done((bf16[256,128]{1,0:T(8,128)(2,1)S(1)}, bf16[256,128]{1,0:T(8,128)(2,1)S(1)}, u32[]{:S(2)}, u32[]{:S(2)}) %collective-permute-start.3) | collective-permute-done | bytes 65568 | tf_op jit(solution)/shard_map/ppermute | solution.py:509
  23.9 3.0 %collective-permute-start.5 = (bf16[256,128]{1,0:T(8,128)(2,1)S(1)}, bf16[256,128]{1,0:T(8,128)(2,1)S(1)}, u32[]{:S(2)}, u32[]{:S(2)}) collective-permute-start(bf16[256,128]{1,0:T(8,128)(2,1)S(1)} %get-tuple-element.45), channel_id=1, source_target_pairs={{0,12},{2,14},{4,8},{6,10},{8,4},{10,6},{12,0},{14,2},{1,13},{3,15... | collective-permute-start | bytes 196616 | tf_op jit(solution)/shard_map/ppermute | solution.py:509
  26.9 0.8 collective-permute-start.6
  27.7 2.2 %collective-permute-done.5.refs_6_.refs_7_ = bf16[256,128]{1,0:T(8,128)(2,1)S(1)} collective-permute-done((bf16[256,128]{1,0:T(8,128)(2,1)S(1)}, bf16[256,128]{1,0:T(8,128)(2,1)S(1)}, u32[]{:S(2)}, u32[]{:S(2)}) %collective-permute-start.5) | collective-permute-done | bytes 65568 | tf_op jit(solution)/shard_map/ppermute | solution.py:509
  29.9 4.0 %collective-permute-done.6.refs_7_.refs_8_ = bf16[256,128]{1,0:T(8,128)(2,1)S(1)} collective-permute-done((bf16[256,128]{1,0:T(8,128)(2,1)S(1)}, bf16[256,128]{1,0:T(8,128)(2,1)S(1)}, u32[]{:S(2)}, u32[]{:S(2)}) %collective-permute-start.6) | collective-permute-done | bytes 65568 | tf_op jit(solution)/shard_map/ppermute | solution.py:509
  34.0 3.6 %shard_map.139 = (f32[128,512]{1,0:T(8,128)S(1)}, f32[8,512]{1,0:T(8,128)S(1)}, bf16[144,512]{1,0:T(8,128)(2,1)S(1)}) custom-call(s32[13]{0:T(128)S(1)} %compare_select_fusion.5.scal, s32[64]{0:T(128)} %row_len.3, bf16[1376,128]{1,0:T(8,128)(2,1)S(1)} %get-tuple-element.39.refs_0_.refs_1_, bf16[1376,128]{1,0:T(8,128)(2,1)S(1)} %collective-permute-done.refs_1_.refs_2_, ...), custom_call_target="tpu_custom_call" | custom-call | tf_op jit(solution)/shard_map/pallas_call | solution.py:599
  38.3 3.6 %shard_map.137 = (f32[128,512]{1,0:T(8,128)S(1)}, f32[8,512]{1,0:T(8,128)S(1)}, bf16[144,512]{1,0:T(8,128)(2,1)S(1)}) custom-call(s32[13]{0:T(128)S(1)} %compare_select_fusion.5.scal, s32[64]{0:T(128)} %row_len.3, bf16[1376,128]{1,0:T(8,128)(2,1)S(1)} %get-tuple-element.39.refs_0_.refs_1_, bf16[1376,128]{1,0:T(8,128)(2,1)S(1)} %collective-permute-done.refs_1_.refs_2_, ...), custom_call_target="tpu_custom_call" | custom-call | tf_op jit(solution)/shard_map/pallas_call | solution.py:599
  41.9 2.4 %collective-permute-start.7 = (bf16[144,512]{1,0:T(8,128)(2,1)S(1)}, bf16[144,512]{1,0:T(8,128)(2,1)S(1)}, u32[]{:S(2)}, u32[]{:S(2)}) collective-permute-start(bf16[144,512]{1,0:T(8,128)(2,1)S(1)} %get-tuple-element.49), channel_id=1, source_target_pairs={{0,8},{2,10},{4,12},{6,14},{8,0},{10,2},{12,4},{14,6},{1,9},{3,11}... | collective-permute-start | bytes 442376 | tf_op jit(solution)/shard_map/ppermute | solution.py:509
  44.3 5.5 %collective-permute-done.8.refs_0_ = bf16[144,512]{1,0:T(8,128)(2,1)S(1)} collective-permute-done((bf16[144,512]{1,0:T(8,128)(2,1)S(1)}, bf16[144,512]{1,0:T(8,128)(2,1)S(1)}, u32[]{:S(2)}, u32[]{:S(2)}) %collective-permute-start.8) | collective-permute-done | bytes 147488 | tf_op jit(solution)/shard_map/ppermute | solution.py:509
  52.0 2.9 %collective-permute-start.14 = (bf16[64,1024]{1,0:T(8,128)(2,1)S(1)}, bf16[64,1024]{1,0:T(8,128)(2,1)S(1)}, u32[]{:S(2)}, u32[]{:S(2)}) collective-permute-start(bf16[64,1024]{1,0:T(8,128)(2,1)S(1)} %shard_map.140.refs_1_), channel_id=1, source_target_pairs={{0,6},{2,4},{4,2},{6,0},{8,14},{10,12},{12,10},{14,8},{1,7},{3,5},... | collective-permute-start | bytes 393224 | tf_op jit(solution)/shard_map/ppermute | solution.py:509
  55.6 2.1 %collective-permute-start.13 = (bf16[64,1024]{1,0:T(8,128)(2,1)S(1)}, bf16[64,1024]{1,0:T(8,128)(2,1)S(1)}, u32[]{:S(2)}, u32[]{:S(2)}) collective-permute-start(bf16[64,1024]{1,0:T(8,128)(2,1)S(1)} %shard_map.138.refs_0_), channel_id=1, source_target_pairs={{0,6},{2,4},{4,2},{6,0},{8,14},{10,12},{12,10},{14,8},{1,7},{3,5},... | collective-permute-start | bytes 393224 | tf_op jit(solution)/shard_map/ppermute | solution.py:509
  57.7 2.7 %collective-permute-done.10.refs_3_ = bf16[64,1024]{1,0:T(8,128)(2,1)S(1)} collective-permute-done((bf16[64,1024]{1,0:T(8,128)(2,1)S(1)}, bf16[64,1024]{1,0:T(8,128)(2,1)S(1)}, u32[]{:S(2)}, u32[]{:S(2)}) %collective-permute-start.10) | collective-permute-done | bytes 131104 | tf_op jit(solution)/shard_map/ppermute | solution.py:509
  60.4 9.5 %shard_map.142 = (bf16[4096,1792]{1,0:T(8,128)(2,1)S(1)}, bf16[4096,1792]{1,0:T(8,128)(2,1)S(1)}) custom-call(bf16[4096,1792]{1,0:T(8,128)(2,1)} %refs_0_.2, bf16[4096,1792]{1,0:T(8,128)(2,1)} %refs_1_.1), custom_call_target="tpu_custom_call" | custom-call | tf_op jit(solution)/shard_map/pallas_call | solution.py:254
  69.9 2.9 %shard_map.143 = (f32[128,3584]{1,0:T(8,128)S(1)}, f32[128,128]{1,0:T(8,128)S(1)}) custom-call(s32[13]{0:T(128)S(1)} %compare_select_fusion.5.scal, bf16[64,1024]{1,0:T(8,128)(2,1)S(1)} %shard_map.138.refs_0_, bf16[64,1024]{1,0:T(8,128)(2,1)S(1)} %shard_map.140.refs_1_, f32[1,4096]{1,0:T(1,128)S(1)} %bitcast.3, ...), custom_call_target="tpu_custom_call" | custom-call | tf_op jit(solution)/shard_map/pallas_call | solution.py:339
  72.8 5.2 %shard_map.144 = (f32[128,3584]{1,0:T(8,128)S(1)}, f32[128,128]{1,0:T(8,128)S(1)}, bf16[128,3712]{1,0:T(8,128)(2,1)S(1)}) custom-call(s32[13]{0:T(128)S(1)} %compare_select_fusion.5.scal, f32[128,3584]{1,0:T(8,128)S(1)} %get-tuple-element.55.refs_0_, f32[128,128]{1,0:T(8,128)S(1)} %get-tuple-element.56.refs_1_, ...), custom_call_target="tpu_custom_call" | custom-call | tf_op jit(solution)/shard_map/pallas_call | solution.py:339
  78.1 5.3 %shard_map.145.refs_3_.refs_1_ = bf16[1792,4096]{1,0:T(8,128)(2,1)S(1)} custom-call(bf16[1792,4096]{1,0:T(8,128)(2,1)} %refs_0_.3), custom_call_target="tpu_custom_call" | custom-call | tf_op jit(solution)/shard_map/pallas_call | solution.py:254
  83.4 2.1 %shard_map.146 = (bf16[128,1792]{1,0:T(8,128)(2,1)S(1)}, f32[32,2048]{1,0:T(8,128)S(1)}, bf16[32,2048]{1,0:T(8,128)(2,1)S(1)}, bf16[32,2048]{1,0:T(8,128)(2,1)S(1)}, bf16[32,2048]{1,0:T(8,128)(2,1)S(1)}) custom-call(s32[13]{0:T(128)S(1)} %compare_select_fusion.5.scal, f32[128,3584]{1,0:T(8,128)S(1)} %get-tuple-element.57.refs_0_, ...), custom_call_target="tpu_custom_call" | custom-call | tf_op jit(solution)/shard_map/pallas_call | solution.py:386
  85.5 1.7 %shard_map.148 = (f32[32,2048]{1,0:T(8,128)S(1)}, bf16[32,2048]{1,0:T(8,128)(2,1)S(1)}, bf16[32,2048]{1,0:T(8,128)(2,1)S(1)}, bf16[32,2048]{1,0:T(8,128)(2,1)S(1)}) custom-call(s32[13]{0:T(128)S(1)} %compare_select_fusion.5.scal, bf16[128,1792]{1,0:T(8,128)(2,1)S(1)} %get-tuple-element.66.refs_0_, bf16[1792,4096]{1,0:T(8,128)(2,1)S(1)} %shard_map.145.refs_3_.refs_1_), custom_call_target="tpu_custom_call" | custom-call | tf_op jit(solution)/shard_map/pallas_call | solution.py:386
  87.2 2.1 %collective-permute-start.20 = (bf16[32,2048]{1,0:T(8,128)(2,1)S(1)}, bf16[32,2048]{1,0:T(8,128)(2,1)S(1)}, u32[]{:S(2)}, u32[]{:S(2)}) collective-permute-start(bf16[32,2048]{1,0:T(8,128)(2,1)S(1)} %get-tuple-element.68), channel_id=1, source_target_pairs={{0,2},{2,0},{4,6},{6,4},{8,10},{10,8},{12,14},{14,12},{1,3},{3,1},... | collective-permute-start | bytes 393224 | tf_op jit(solution)/shard_map/ppermute | solution.py:509
  89.3 1.5 %collective-permute-start.22 = (bf16[32,2048]{1,0:T(8,128)(2,1)S(1)}, bf16[32,2048]{1,0:T(8,128)(2,1)S(1)}, u32[]{:S(2)}, u32[]{:S(2)}) collective-permute-start(bf16[32,2048]{1,0:T(8,128)(2,1)S(1)} %get-tuple-element.70), channel_id=1, source_target_pairs={{0,6},{2,4},{4,2},{6,0},{8,14},{10,12},{12,10},{14,8},{1,7},{3,5},... | collective-permute-start | bytes 393224 | tf_op jit(solution)/shard_map/ppermute | solution.py:509
  90.8 1.9 %collective-permute-start.16 = (bf16[32,2048]{1,0:T(8,128)(2,1)S(1)}, bf16[32,2048]{1,0:T(8,128)(2,1)S(1)}, u32[]{:S(2)}, u32[]{:S(2)}) collective-permute-start(bf16[32,2048]{1,0:T(8,128)(2,1)S(1)} %get-tuple-element.61), channel_id=1, source_target_pairs={{0,2},{2,0},{4,6},{6,4},{8,10},{10,8},{12,14},{14,12},{1,3},{3,1},... | collective-permute-start | bytes 393224 | tf_op jit(solution)/shard_map/ppermute | solution.py:509
  93.5 0.8 collective-permute-start.18
  94.3 1.3 %collective-permute-done.21.refs_2_ = bf16[32,2048]{1,0:T(8,128)(2,1)S(1)} collective-permute-done((bf16[32,2048]{1,0:T(8,128)(2,1)S(1)}, bf16[32,2048]{1,0:T(8,128)(2,1)S(1)}, u32[]{:S(2)}, u32[]{:S(2)}) %collective-permute-start.21) | collective-permute-done | bytes 131104 | tf_op jit(solution)/shard_map/ppermute | solution.py:509
  95.7 2.4 %collective-permute-done.22.refs_3_ = bf16[32,2048]{1,0:T(8,128)(2,1)S(1)} collective-permute-done((bf16[32,2048]{1,0:T(8,128)(2,1)S(1)}, bf16[32,2048]{1,0:T(8,128)(2,1)S(1)}, u32[]{:S(2)}, u32[]{:S(2)}) %collective-permute-start.22) | collective-permute-done | bytes 131104 | tf_op jit(solution)/shard_map/ppermute | solution.py:509
  99.1 2.3 %collective-permute-done.17.refs_2_ = bf16[32,2048]{1,0:T(8,128)(2,1)S(1)} collective-permute-done((bf16[32,2048]{1,0:T(8,128)(2,1)S(1)}, bf16[32,2048]{1,0:T(8,128)(2,1)S(1)}, u32[]{:S(2)}, u32[]{:S(2)}) %collective-permute-start.17) | collective-permute-done | bytes 131104 | tf_op jit(solution)/shard_map/ppermute | solution.py:509
  101.3 2.6 %collective-permute-done.18.refs_3_ = bf16[32,2048]{1,0:T(8,128)(2,1)S(1)} collective-permute-done((bf16[32,2048]{1,0:T(8,128)(2,1)S(1)}, bf16[32,2048]{1,0:T(8,128)(2,1)S(1)}, u32[]{:S(2)}, u32[]{:S(2)}) %collective-permute-start.18) | collective-permute-done | bytes 131104 | tf_op jit(solution)/shard_map/ppermute | solution.py:509
  105.3 4.8 %collective-permute-done.19 = bf16[16,2048]{1,0:T(8,128)(2,1)S(1)} collective-permute-done((bf16[16,2048]{1,0:T(8,128)(2,1)S(1)}, bf16[16,2048]{1,0:T(8,128)(2,1)S(1)}, u32[]{:S(2)}, u32[]{:S(2)}) %collective-permute-start.19) | collective-permute-done | bytes 65568 | tf_op jit(solution)/shard_map/ppermute | solution.py:509
  (38 shorter events, 7.7 us)
Async XLA Ops:
  2.4 31.6 %collective-permute-start = (bf16[1376,128]{1,0:T(8,128)(2,1)S(1)}, bf16[1376,128]{1,0:T(8,128)(2,1)S(1)}, u32[]{:S(2)}, u32[]{:S(2)}) collective-permute-start(bf16[1376,128]{1,0:T(8,128)(2,1)S(1)} %get-tuple-element.40), channel_id=1, source_target_pairs={{0,2},{2,0},{4,6},{6,4},{8,10},{10,8},{12,14},{14,12},{1,3},{3,1},... | collective-permute-start | bytes 1056776 | tf_op jit(solution)/shard_map/ppermute | solution.py:509
  5.4 28.5 %collective-permute-start.1 = (bf16[1376,128]{1,0:T(8,128)(2,1)S(1)}, bf16[1376,128]{1,0:T(8,128)(2,1)S(1)}, u32[]{:S(2)}, u32[]{:S(2)}) collective-permute-start(bf16[1376,128]{1,0:T(8,128)(2,1)S(1)} %get-tuple-element.41), channel_id=1, source_target_pairs={{0,4},{2,6},{4,0},{6,2},{8,12},{10,14},{12,8},{14,10},{1,5},{3,7},... | collective-permute-start | bytes 1056776 | tf_op jit(solution)/shard_map/ppermute | solution.py:509
  7.0 27.0 %collective-permute-start.2 = (bf16[1376,128]{1,0:T(8,128)(2,1)S(1)}, bf16[1376,128]{1,0:T(8,128)(2,1)S(1)}, u32[]{:S(2)}, u32[]{:S(2)}) collective-permute-start(bf16[1376,128]{1,0:T(8,128)(2,1)S(1)} %get-tuple-element.42), channel_id=1, source_target_pairs={{0,6},{2,4},{4,2},{6,0},{8,14},{10,12},{12,10},{14,8},{1,7},{3,5},... | collective-permute-start | bytes 1056776 | tf_op jit(solution)/shard_map/ppermute | solution.py:509
  7.0 16.9 %collective-permute-start.3 = (bf16[256,128]{1,0:T(8,128)(2,1)S(1)}, bf16[256,128]{1,0:T(8,128)(2,1)S(1)}, u32[]{:S(2)}, u32[]{:S(2)}) collective-permute-start(bf16[256,128]{1,0:T(8,128)(2,1)S(1)} %get-tuple-element.43), channel_id=1, source_target_pairs={{0,8},{2,10},{4,12},{6,14},{8,0},{10,2},{12,4},{14,6},{1,9},{3,11}... | collective-permute-start | bytes 196616 | tf_op jit(solution)/shard_map/ppermute | solution.py:509
  10.0 16.9 %collective-permute-start.4 = (bf16[256,128]{1,0:T(8,128)(2,1)S(1)}, bf16[256,128]{1,0:T(8,128)(2,1)S(1)}, u32[]{:S(2)}, u32[]{:S(2)}) collective-permute-start(bf16[256,128]{1,0:T(8,128)(2,1)S(1)} %get-tuple-element.44), channel_id=1, source_target_pairs={{0,10},{2,8},{4,14},{6,12},{8,2},{10,0},{12,6},{14,4},{1,11},{3,9}... | collective-permute-start | bytes 196616 | tf_op jit(solution)/shard_map/ppermute | solution.py:509
  23.9 6.1 %collective-permute-start.5 = (bf16[256,128]{1,0:T(8,128)(2,1)S(1)}, bf16[256,128]{1,0:T(8,128)(2,1)S(1)}, u32[]{:S(2)}, u32[]{:S(2)}) collective-permute-start(bf16[256,128]{1,0:T(8,128)(2,1)S(1)} %get-tuple-element.45), channel_id=1, source_target_pairs={{0,12},{2,14},{4,8},{6,10},{8,4},{10,6},{12,0},{14,2},{1,13},{3,15... | collective-permute-start | bytes 196616 | tf_op jit(solution)/shard_map/ppermute | solution.py:509
  26.9 7.1 %collective-permute-start.6 = (bf16[256,128]{1,0:T(8,128)(2,1)S(1)}, bf16[256,128]{1,0:T(8,128)(2,1)S(1)}, u32[]{:S(2)}, u32[]{:S(2)}) collective-permute-start(bf16[256,128]{1,0:T(8,128)(2,1)S(1)} %get-tuple-element.46), channel_id=1, source_target_pairs={{0,14},{2,12},{4,10},{6,8},{8,6},{10,4},{12,2},{14,0},{1,15},{3,13... | collective-permute-start | bytes 196616 | tf_op jit(solution)/shard_map/ppermute | solution.py:509
  37.6 12.2 %collective-permute-start.8 = (bf16[144,512]{1,0:T(8,128)(2,1)S(1)}, bf16[144,512]{1,0:T(8,128)(2,1)S(1)}, u32[]{:S(2)}, u32[]{:S(2)}) collective-permute-start(bf16[144,512]{1,0:T(8,128)(2,1)S(1)} %get-tuple-element.52), channel_id=1, source_target_pairs={{0,8},{2,10},{4,12},{6,14},{8,0},{10,2},{12,4},{14,6},{1,9},{3,11}... | collective-permute-start | bytes 442376 | tf_op jit(solution)/shard_map/ppermute | solution.py:509
  41.9 12.9 %collective-permute-start.7 = (bf16[144,512]{1,0:T(8,128)(2,1)S(1)}, bf16[144,512]{1,0:T(8,128)(2,1)S(1)}, u32[]{:S(2)}, u32[]{:S(2)}) collective-permute-start(bf16[144,512]{1,0:T(8,128)(2,1)S(1)} %get-tuple-element.49), channel_id=1, source_target_pairs={{0,8},{2,10},{4,12},{6,14},{8,0},{10,2},{12,4},{14,6},{1,9},{3,11}... | collective-permute-start | bytes 442376 | tf_op jit(solution)/shard_map/ppermute | solution.py:509
  49.8 0.7 copy-start
  51.3 9.1 %collective-permute-start.10 = (bf16[64,1024]{1,0:T(8,128)(2,1)S(1)}, bf16[64,1024]{1,0:T(8,128)(2,1)S(1)}, u32[]{:S(2)}, u32[]{:S(2)}) collective-permute-start(bf16[64,1024]{1,0:T(8,128)(2,1)S(1)} %shard_map.140.refs_1_), channel_id=1, source_target_pairs={{0,2},{2,0},{4,6},{6,4},{8,10},{10,8},{12,14},{14,12},{1,3},{3,1},... | collective-permute-start | bytes 393224 | tf_op jit(solution)/shard_map/ppermute | solution.py:509
  51.9 20.8 %collective-permute-start.12 = (bf16[64,1024]{1,0:T(8,128)(2,1)S(1)}, bf16[64,1024]{1,0:T(8,128)(2,1)S(1)}, u32[]{:S(2)}, u32[]{:S(2)}) collective-permute-start(bf16[64,1024]{1,0:T(8,128)(2,1)S(1)} %shard_map.140.refs_1_), channel_id=1, source_target_pairs={{0,4},{2,6},{4,0},{6,2},{8,12},{10,14},{12,8},{14,10},{1,5},{3,7},... | collective-permute-start | bytes 393224 | tf_op jit(solution)/shard_map/ppermute | solution.py:509
  52.0 20.8 %collective-permute-start.14 = (bf16[64,1024]{1,0:T(8,128)(2,1)S(1)}, bf16[64,1024]{1,0:T(8,128)(2,1)S(1)}, u32[]{:S(2)}, u32[]{:S(2)}) collective-permute-start(bf16[64,1024]{1,0:T(8,128)(2,1)S(1)} %shard_map.140.refs_1_), channel_id=1, source_target_pairs={{0,6},{2,4},{4,2},{6,0},{8,14},{10,12},{12,10},{14,8},{1,7},{3,5},... | collective-permute-start | bytes 393224 | tf_op jit(solution)/shard_map/ppermute | solution.py:509
  55.5 14.3 %copy-start.1 = (f32[4096]{0:T(1024)S(1)}, f32[4096]{0:T(1024)}, u32[]{:S(2)}) copy-start(f32[4096]{0:T(1024)} %param.24) | copy-start | bytes 49156
  55.6 17.3 %collective-permute-start.11 = (bf16[64,1024]{1,0:T(8,128)(2,1)S(1)}, bf16[64,1024]{1,0:T(8,128)(2,1)S(1)}, u32[]{:S(2)}, u32[]{:S(2)}) collective-permute-start(bf16[64,1024]{1,0:T(8,128)(2,1)S(1)} %shard_map.138.refs_0_), channel_id=1, source_target_pairs={{0,4},{2,6},{4,0},{6,2},{8,12},{10,14},{12,8},{14,10},{1,5},{3,7},... | collective-permute-start | bytes 393224 | tf_op jit(solution)/shard_map/ppermute | solution.py:509
  55.6 17.2 %collective-permute-start.13 = (bf16[64,1024]{1,0:T(8,128)(2,1)S(1)}, bf16[64,1024]{1,0:T(8,128)(2,1)S(1)}, u32[]{:S(2)}, u32[]{:S(2)}) collective-permute-start(bf16[64,1024]{1,0:T(8,128)(2,1)S(1)} %shard_map.138.refs_0_), channel_id=1, source_target_pairs={{0,6},{2,4},{4,2},{6,0},{8,14},{10,12},{12,10},{14,8},{1,7},{3,5},... | collective-permute-start | bytes 393224 | tf_op jit(solution)/shard_map/ppermute | solution.py:509
  60.4 12.5 %collective-permute-start.9 = (bf16[64,1024]{1,0:T(8,128)(2,1)S(1)}, bf16[64,1024]{1,0:T(8,128)(2,1)S(1)}, u32[]{:S(2)}, u32[]{:S(2)}) collective-permute-start(bf16[64,1024]{1,0:T(8,128)(2,1)S(1)} %shard_map.138.refs_0_), channel_id=1, source_target_pairs={{0,2},{2,0},{4,6},{6,4},{8,10},{10,8},{12,14},{14,12},{1,3},{3,1},... | collective-permute-start | bytes 393224 | tf_op jit(solution)/shard_map/ppermute | solution.py:509
  78.0 5.4 %collective-permute-start.15 = (bf16[128,3712]{1,0:T(8,128)(2,1)S(1)}, bf16[128,3712]{1,0:T(8,128)(2,1)S(1)}, u32[]{:S(2)}, u32[]{:S(2)}) collective-permute-start(bf16[128,3712]{1,0:T(8,128)(2,1)S(1)} %get-tuple-element.59), channel_id=1, source_target_pairs={{0,1},{1,0},{2,3},{3,2},{4,5},{5,4},{6,7},{7,6},{8,9},{9,8},{10,11... | collective-permute-start | bytes 2850824 | tf_op jit(solution)/shard_map/ppermute | solution.py:622
  87.2 6.3 %collective-permute-start.20 = (bf16[32,2048]{1,0:T(8,128)(2,1)S(1)}, bf16[32,2048]{1,0:T(8,128)(2,1)S(1)}, u32[]{:S(2)}, u32[]{:S(2)}) collective-permute-start(bf16[32,2048]{1,0:T(8,128)(2,1)S(1)} %get-tuple-element.68), channel_id=1, source_target_pairs={{0,2},{2,0},{4,6},{6,4},{8,10},{10,8},{12,14},{14,12},{1,3},{3,1},... | collective-permute-start | bytes 393224 | tf_op jit(solution)/shard_map/ppermute | solution.py:509
  89.3 6.4 %collective-permute-start.21 = (bf16[32,2048]{1,0:T(8,128)(2,1)S(1)}, bf16[32,2048]{1,0:T(8,128)(2,1)S(1)}, u32[]{:S(2)}, u32[]{:S(2)}) collective-permute-start(bf16[32,2048]{1,0:T(8,128)(2,1)S(1)} %get-tuple-element.69), channel_id=1, source_target_pairs={{0,4},{2,6},{4,0},{6,2},{8,12},{10,14},{12,8},{14,10},{1,5},{3,7},... | collective-permute-start | bytes 393224 | tf_op jit(solution)/shard_map/ppermute | solution.py:509
  89.3 8.7 %collective-permute-start.22 = (bf16[32,2048]{1,0:T(8,128)(2,1)S(1)}, bf16[32,2048]{1,0:T(8,128)(2,1)S(1)}, u32[]{:S(2)}, u32[]{:S(2)}) collective-permute-start(bf16[32,2048]{1,0:T(8,128)(2,1)S(1)} %get-tuple-element.70), channel_id=1, source_target_pairs={{0,6},{2,4},{4,2},{6,0},{8,14},{10,12},{12,10},{14,8},{1,7},{3,5},... | collective-permute-start | bytes 393224 | tf_op jit(solution)/shard_map/ppermute | solution.py:509
  90.8 8.2 %collective-permute-start.16 = (bf16[32,2048]{1,0:T(8,128)(2,1)S(1)}, bf16[32,2048]{1,0:T(8,128)(2,1)S(1)}, u32[]{:S(2)}, u32[]{:S(2)}) collective-permute-start(bf16[32,2048]{1,0:T(8,128)(2,1)S(1)} %get-tuple-element.61), channel_id=1, source_target_pairs={{0,2},{2,0},{4,6},{6,4},{8,10},{10,8},{12,14},{14,12},{1,3},{3,1},... | collective-permute-start | bytes 393224 | tf_op jit(solution)/shard_map/ppermute | solution.py:509
  92.8 8.5 %collective-permute-start.17 = (bf16[32,2048]{1,0:T(8,128)(2,1)S(1)}, bf16[32,2048]{1,0:T(8,128)(2,1)S(1)}, u32[]{:S(2)}, u32[]{:S(2)}) collective-permute-start(bf16[32,2048]{1,0:T(8,128)(2,1)S(1)} %get-tuple-element.62), channel_id=1, source_target_pairs={{0,4},{2,6},{4,0},{6,2},{8,12},{10,14},{12,8},{14,10},{1,5},{3,7},... | collective-permute-start | bytes 393224 | tf_op jit(solution)/shard_map/ppermute | solution.py:509
  93.5 10.3 %collective-permute-start.18 = (bf16[32,2048]{1,0:T(8,128)(2,1)S(1)}, bf16[32,2048]{1,0:T(8,128)(2,1)S(1)}, u32[]{:S(2)}, u32[]{:S(2)}) collective-permute-start(bf16[32,2048]{1,0:T(8,128)(2,1)S(1)} %get-tuple-element.63), channel_id=1, source_target_pairs={{0,6},{2,4},{4,2},{6,0},{8,14},{10,12},{12,10},{14,8},{1,7},{3,5},... | collective-permute-start | bytes 393224 | tf_op jit(solution)/shard_map/ppermute | solution.py:509
  98.7 6.6 %collective-permute-start.23 = (bf16[16,2048]{1,0:T(8,128)(2,1)S(1)}, bf16[16,2048]{1,0:T(8,128)(2,1)S(1)}, u32[]{:S(2)}, u32[]{:S(2)}) collective-permute-start(bf16[16,2048]{1,0:T(8,128)(2,1)S(1)} %get-tuple-element.72), channel_id=1, source_target_pairs={{0,8},{2,10},{4,12},{6,14},{8,0},{10,2},{12,4},{14,6},{1,9},{3,11}... | collective-permute-start | bytes 196616 | tf_op jit(solution)/shard_map/ppermute | solution.py:509
  104.5 5.7 %collective-permute-start.19 = (bf16[16,2048]{1,0:T(8,128)(2,1)S(1)}, bf16[16,2048]{1,0:T(8,128)(2,1)S(1)}, u32[]{:S(2)}, u32[]{:S(2)}) collective-permute-start(bf16[16,2048]{1,0:T(8,128)(2,1)S(1)} %get-tuple-element.65), channel_id=1, source_target_pairs={{0,8},{2,10},{4,12},{6,14},{8,0},{10,2},{12,4},{14,6},{1,9},{3,11}... | collective-permute-start | bytes 196616 | tf_op jit(solution)/shard_map/ppermute | solution.py:509

commit v2 on v1

--- a/solution.py
+++ b/solution.py
@@ -95,26 +95,27 @@
 
 
 def attention_kernel(dims, scal, row_len, *refs):
-    hs, n, span, pages, rows, tl, steps, first_source, count = dims
+    hs, _, span, pages, rows, tl, steps, group = dims
     blocks = refs[:hs]
-    crosses = refs[hs:n]
-    acc_ref, stat_ref, send_ref, qs, ks, vs, fk, fv, scale, lens_ref = refs[n:]
+    q_refs, refs = (blocks, refs[hs:]) if group == 0 else (refs[hs : 2 * hs], refs[2 * hs :])
+    acc_ref, stat_ref, send_ref, qs, ks, vs, fk, fv, scale, lens_ref = refs
     hd = ks.shape[1]
     blk = span // pages
-    nq = count * rows
+    nq = hs * rows
     q_at = 2 * span + META * pages
     inv_root = LOG2E / math.sqrt(hd)
-    for d in range(n):
-        ref, at = (blocks[d], q_at) if d < hs else (crosses[d - hs], 0)
-        start = pl.multiple_of(scal[d] * rows, rows)
-        qs[pl.ds(start, rows), :] = ref[at : at + rows, :]
+    for d in range(hs):
+        at = q_at if group == 0 else 0
+        start = pl.multiple_of(lax.rem(scal[d], hs) * rows, rows)
+        qs[pl.ds(start, rows), :] = q_refs[d][at : at + rows, :]
     f_at = q_at + 2 * rows
     fresh = fk.shape[0] // hs
     for d in range(hs):
         ks[d * span : (d + 1) * span, :] = blocks[d][0:span, :]
         vs[d * span : (d + 1) * span, :] = blocks[d][span : 2 * span, :]
-        fk[d * fresh : (d + 1) * fresh, :] = blocks[d][f_at : f_at + fresh, :]
-        fv[d * fresh : (d + 1) * fresh, :] = blocks[d][f_at + fresh : f_at + 2 * fresh, :]
+        if group == 0:
+            fk[d * fresh : (d + 1) * fresh, :] = blocks[d][f_at : f_at + fresh, :]
+            fv[d * fresh : (d + 1) * fresh, :] = blocks[d][f_at + fresh : f_at + 2 * fresh, :]
         meta = blocks[d][2 * span : 2 * span + META * pages, :].astype(F32)
         for page in range(pages):
             m = meta[page * META : (page + 1) * META, :]
@@ -123,19 +124,18 @@
             at = (d * pages + page) * META
             scale[at : at + META, :] = jnp.concatenate([k_row, v_row, m[6:7] * float(blk), m[3:8]], axis=0)
     lanes = min(256, nq)
-    base_q = first_source * rows
     lane = lax.broadcasted_iota(jnp.int32, (1, nq), 1)
     rl = tl // steps
     lane_row = (lane // rows) * rl + (lane % tl) // steps
     lens = jnp.zeros((1, nq), F32)
-    for j in range(count * rl):
-        lens = jnp.where(lane_row == j, row_len[first_source * rl + j].astype(F32), lens)
+    half = scal[group * hs] // hs
+    for j in range(hs * rl):
+        lens = jnp.where(lane_row == j, row_len[half * (hs * rl) + j].astype(F32), lens)
     lens_ref[...] = lens
 
     def chunk(c, carry):
         at = pl.multiple_of(c * lanes, lanes)
-        at_q = pl.multiple_of(base_q + c * lanes, lanes)
-        q = qs[pl.ds(at_q, lanes), :]
+        q = qs[pl.ds(at, lanes), :]
         length = lens_ref[0:1, pl.ds(at, lanes)]
         raw = lax.dot_general(ks[...], q, NT, preferred_element_type=F32)
         inner = lax.broadcasted_iota(jnp.int32, (blk, lanes), 0).astype(F32)
@@ -145,24 +145,29 @@
             limit = length - scale[page * META + 2 : page * META + 3, 0:1]
             part = raw[page * blk : (page + 1) * blk, :] * k_scale
             scores.append(jnp.where(inner < limit, part, NEG_FILL))
-        lane = lax.broadcasted_iota(jnp.int32, (1, lanes), 1) + at_q
-        source = lane // rows
-        token = lane % tl
-        fi = lax.broadcasted_iota(jnp.int32, (fk.shape[0], 1), 0)
-        f_slot = fi // fresh
-        f_token = fi % fresh
-        f_source = jnp.where(f_token < tl, scal[0], -1)
-        for d in range(1, hs):
-            f_source = jnp.where((f_slot == d) & (f_token < tl), scal[d], f_source)
-        keep = (f_source == source) & (f_token // steps == token // steps) & (f_token % steps <= token % steps)
-        raw_f = lax.dot_general(fk[...], q, NT, preferred_element_type=F32) * inv_root
-        fresh_scores = jnp.where(keep, raw_f, NEG_FILL)
-        top = jnp.max(fresh_scores, axis=0, keepdims=True)
+        top = jnp.full((1, lanes), TOP_FLOOR, F32)
+        if group == 0:
+            lane = lax.broadcasted_iota(jnp.int32, (1, lanes), 1) + at
+            source = lane // rows
+            token = lane % tl
+            fi = lax.broadcasted_iota(jnp.int32, (fk.shape[0], 1), 0)
+            f_slot = fi // fresh
+            f_token = fi % fresh
+            f_source = jnp.full((fk.shape[0], 1), -1, jnp.int32)
+            for d in range(hs):
+                f_source = jnp.where((f_slot == d) & (f_token < tl), lax.rem(scal[d], hs), f_source)
+            keep = (f_source == source) & (f_token // steps == token // steps)
+            keep = keep & (f_token % steps <= token % steps)
+            raw_f = lax.dot_general(fk[...], q, NT, preferred_element_type=F32) * inv_root
+            fresh_scores = jnp.where(keep, raw_f, NEG_FILL)
+            top = jnp.maximum(top, jnp.max(fresh_scores, axis=0, keepdims=True))
         for part in scores:
             top = jnp.maximum(top, jnp.max(part, axis=0, keepdims=True))
-        top = jnp.maximum(jnp.ceil(top), TOP_FLOOR)
-        fresh_terms = jnp.exp2(fresh_scores - top)
-        total = jnp.sum(fresh_terms, axis=0, keepdims=True)
+        top = jnp.ceil(top)
+        total = jnp.zeros((1, lanes), F32)
+        if group == 0:
+            fresh_terms = jnp.exp2(fresh_scores - top)
+            total = jnp.sum(fresh_terms, axis=0, keepdims=True)
         weights = []
         for page, part in enumerate(scores):
             terms = jnp.exp2(part - top)
@@ -170,7 +175,8 @@
             weights.append((terms * scale[page * META + 1 : page * META + 2, 0:1]).astype(BF))
         weight = jnp.concatenate(weights, axis=0)
         acc = lax.dot_general(vs[...], weight, TN, preferred_element_type=F32)
-        acc = acc + lax.dot_general(fv[...], fresh_terms.astype(BF), TN, preferred_element_type=F32)
+        if group == 0:
+            acc = acc + lax.dot_general(fv[...], fresh_terms.astype(BF), TN, preferred_element_type=F32)
         acc_ref[:, pl.ds(at, lanes)] = acc
         send_ref[0:hd, pl.ds(at, lanes)] = acc.astype(BF)
         zero = jnp.zeros((1, lanes), F32)
@@ -188,19 +194,15 @@
 
 
 def combine_kernel(dims, scal, acc_ref, stat_ref, gain_ref, *refs):
-    hs, r, rows, tl, aligned, res_at, first_source, count = dims
-    n = hs * r
+    hs, r, rows, tl, aligned, res_at = dims
     received = refs[: r - 1]
-    blocks = refs[r - 1 : r - 1 + hs]
-    crosses = refs[r - 1 + hs : r - 1 + n]
-    out_ref, res = refs[r - 1 + n :]
+    sources = refs[r - 1 : r - 1 + hs]
+    out_ref, res = refs[r - 1 + hs :]
     hd = acc_ref.shape[0]
     hp = rows // tl
-    per = count // hs
-    for d in range(n):
-        ref, at = (blocks[d], res_at) if d < hs else (crosses[d - hs], rows)
-        start = pl.multiple_of(scal[d] * rows, rows)
-        res[pl.ds(start, rows), :] = ref[at : at + rows, :]
+    for d in range(hs):
+        start = pl.multiple_of(lax.rem(scal[d], hs) * rows, rows)
+        res[pl.ds(start, rows), :] = sources[d][res_at : res_at + rows, :]
     top = stat_ref[0:1, :]
     total = stat_ref[1:2, :]
     others = []
@@ -221,11 +223,9 @@
         value = value + ref[0:hd, :].astype(F32) * (jnp.exp2(o_top - best) / total)
     width = hp * hd
     gain = gain_ref[0:1, pl.ds(pl.multiple_of(lax.rem(scal[0], hs) * width, width), width)]
-    for s in range(count):
-        part = value[:, s * rows : (s + 1) * rows].T
-        at = (first_source + s) * rows
-        part = part + res[at : at + rows, :].astype(F32)
-        slot = (s % hs) * per + s // hs
+    for slot in range(hs):
+        at = slot * rows
+        part = value[:, at : at + rows].T + res[at : at + rows, :].astype(F32)
         heads = [part[h * tl : (h + 1) * tl, :] * gain[:, h * hd : (h + 1) * hd] for h in range(hp)]
         if aligned:
             for h in range(hp):
@@ -257,7 +257,7 @@
         in_specs=[HBM] * count,
         out_specs=[VMEM] * count,
         scratch_shapes=[pltpu.SemaphoreType.DMA((count, pieces))],
-        compiler_params=params(1),
+        compiler_params=pltpu.CompilerParams(vmem_limit_bytes=(8 << 20) + 4096),
     )(*[hbm(x) for x in arrays])
 
 
@@ -342,7 +342,7 @@
         in_specs=[SMEM] + [VMEM] * len(args),
         out_specs=[VMEM] * len(out_shape),
         scratch_shapes=[pltpu.VMEM((len(offsets), tokens, width), BF)],
-        compiler_params=params(4),
+        compiler_params=params(8),
     )(scal, *args)
 
 
@@ -365,15 +365,23 @@
     block = tokens // (hs * groups)
     tile = scratch.shape[1]
     for c in range(width // tile):
-        scratch[...] = jnp.dot(
+        value = jnp.dot(
             hidden[...], wd_ref[:, offset + c * tile : offset + (c + 1) * tile], preferred_element_type=F32
         )
+        if block % 8 == 0:
+            scratch[...] = value
         for d in range(hs):
             for g in range(groups):
-                at = pl.multiple_of(g * (tokens // groups) + scal[n + d] * block, block)
-                pieces[d][g * block : (g + 1) * block, c * tile : (c + 1) * tile] = scratch[
-                    pl.ds(at, block), :
-                ].astype(pieces[d].dtype)
+                first_row = g * (tokens // groups)
+                if block % 8 == 0:
+                    at = pl.multiple_of(first_row + scal[n + d] * block, block)
+                    piece = scratch[pl.ds(at, block), :]
+                else:
+                    piece = value[first_row : first_row + block, :]
+                    for j in range(1, hs):
+                        at = first_row + j * block
+                        piece = jnp.where(scal[n + d] == j, value[at : at + block, :], piece)
+                pieces[d][g * block : (g + 1) * block, c * tile : (c + 1) * tile] = piece.astype(pieces[d].dtype)
 
 
 def down(first, n, hs, groups, scal, args, w_down, offset, width, model):
@@ -394,65 +402,48 @@
 
 
 def own_kernel(dims, scal, gain_ref, *refs):
-    n, hs, groups, tl = dims
+    n, hs, tl = dims
     parts, out_ref = refs[:-1], refs[-1]
-    per, width = parts[0].shape
-    index = scal[n + hs]
-    a = lax.rem(index, hs)
-    b = index // hs
-    rc = n // hs // groups
-    slot = (b // rc) * (per // tl) + a * rc + lax.rem(b, rc)
+    width = parts[0].shape[1]
+    a = lax.rem(scal[n + hs], hs)
     for d in range(hs):
-        h = jnp.zeros((tl, width), F32)
-        for g in range(groups):
-            part = parts[d * groups + g][...].astype(F32)
-            for j in range(per // tl):
-                take = slot == g * (per // tl) + j
-                h = jnp.where(take, part[j * tl : (j + 1) * tl, :], h)
+        part = parts[d][...].astype(F32)
+        h = part[0:tl, :]
+        for j in range(1, hs):
+            h = jnp.where(a == j, part[j * tl : (j + 1) * tl, :], h)
         start = pl.multiple_of(lax.rem(scal[d], hs) * width, width)
         out_ref[:, pl.ds(start, width)] = h / gain_ref[0:1, pl.ds(start, width)]
 
 
-def own_state(scal, gain, parts, n, hs, groups, tl):
+def own_state(scal, gain, parts, n, hs, tl):
     half = gain.shape[1]
     return pl.pallas_call(
-        functools.partial(own_kernel, (n, hs, groups, tl)),
+        functools.partial(own_kernel, (n, hs, tl)),
         out_shape=jax.ShapeDtypeStruct((tl, half), F32),
         in_specs=[SMEM] + [VMEM] * (1 + len(parts)),
         out_specs=VMEM,
-        compiler_params=params(8),
+        compiler_params=params(4),
     )(scal, gain, *parts)
 
 
-def square_sum_kernel(dims, scal, *refs):
-    n, hs, r, tl = dims
-    pieces, mine, aways = refs[:hs], refs[hs], refs[hs + 1 :]
-    b = scal[n + hs] // hs
+def square_sum_kernel(r, tl, *refs):
+    pieces, outs = refs[:-r], refs[-r:]
     total = pieces[0][...]
     for ref in pieces[1:]:
         total = total + ref[...].astype(F32)
-    rows = [total[j * tl : (j + 1) * tl, :] for j in range(r)]
     for db in range(r):
-        want = lax.rem(b + db, r)
-        value = rows[0]
-        for j in range(1, r):
-            value = jnp.where(want == j, rows[j], value)
-        if db == 0:
-            mine[...] = value
-        else:
-            aways[db - 1][...] = value.astype(BF)
-
-
-def square_sum(scal, pieces, n, hs, r, tl):
+        outs[db][...] = total[db * tl : (db + 1) * tl, :].astype(outs[db].dtype)
+
+
+def square_sum(pieces, r, tl):
     width = pieces[0].shape[1]
     return pl.pallas_call(
-        functools.partial(square_sum_kernel, (n, hs, r, tl)),
-        out_shape=[jax.ShapeDtypeStruct((tl, width), F32)]
-        + [jax.ShapeDtypeStruct((tl, width), BF)] * (r - 1),
-        in_specs=[SMEM] + [VMEM] * hs,
+        functools.partial(square_sum_kernel, r, tl),
+        out_shape=[jax.ShapeDtypeStruct((tl, width), F32 if db == 0 else BF) for db in range(r)],
+        in_specs=[VMEM] * len(pieces),
         out_specs=[VMEM] * r,
-        compiler_params=params(8),
-    )(scal, *pieces)
+        compiler_params=params(4),
+    )(*pieces)
 
 
 def make_body(n):
@@ -481,13 +472,10 @@
         r = n // hs
         tl = rl * steps
         rows = hp * tl
-        nq = n * rows
         width = hp * hd
         ffl = w_gate.shape[1]
         ffp = round_up(ffl, 128)
         model = half * 2
-        groups = 2 if r % 2 == 0 else 1
-        count = n // groups
         aligned = tl % 16 == 0
         fpad = round_up(tl, 16)
         index = lax.axis_index("seq")
@@ -522,7 +510,7 @@
                 in_specs=[SMEM] * 4 + [VMEM] * 4 + [HBM] * 2,
                 out_specs=[VMEM] * (2 * hs),
                 scratch_shapes=[pltpu.SemaphoreType.DMA((hs, 2))],
-                compiler_params=params(8),
+                compiler_params=params(4),
             )(
                 scal,
                 *[
@@ -571,22 +559,21 @@
         wg, wu = prefetch(w_gate, w_up)
         gain2 = norm_gain.reshape(1, half)
         res_at = 2 * span + META * pages + rows
-        nc = count * rows
+        nc = hs * rows
+        per = hs * tl
         partial = []
-        for g in range(groups):
+        for g in range(r):
             attend = pl.pallas_call(
-                functools.partial(
-                    attention_kernel, (hs, n, span, pages, rows, tl, steps, g * count, count)
-                ),
+                functools.partial(attention_kernel, (hs, n, span, pages, rows, tl, steps, g)),
                 out_shape=(
                     jax.ShapeDtypeStruct((hd, nc), F32),
                     jax.ShapeDtypeStruct((8, nc), F32),
                     jax.ShapeDtypeStruct((hd + 16, nc), BF),
                 ),
-                in_specs=[SMEM, SMEM] + [VMEM] * n,
+                in_specs=[SMEM, SMEM] + [VMEM] * (hs if g == 0 else 2 * hs),
                 out_specs=(VMEM, VMEM, VMEM),
                 scratch_shapes=[
-                    pltpu.VMEM((nq, hd), BF),
+                    pltpu.VMEM((nc, hd), BF),
                     pltpu.VMEM((hs * span, hd), BF),
                     pltpu.VMEM((hs * span, hd), BF),
                     pltpu.VMEM((hs * fpad, hd), BF),
@@ -594,26 +581,32 @@
                     pltpu.VMEM((hs * pages * META, hd), F32),
                     pltpu.VMEM((1, nc), F32),
                 ],
-                compiler_params=params(8 if aligned else 16),
+                compiler_params=params(4 if aligned else 16),
             )
-            acc, stat, sent = attend(scal, hbm(row_lengths), *blocks, *crosses)
-            partial.append((acc, stat, [shift(sent, db, 0) for db in range(1, r)]))
-        per = count * tl
-        mine = []
-        for g, (acc, stat, received) in enumerate(partial):
-            p_shape = (per, width) if aligned else (count, rows, hd)
+            extra = [] if g == 0 else crosses[(g - 1) * hs : g * hs]
+            partial.append(attend(scal, hbm(row_lengths), *blocks, *extra))
+        mine = [None] * r
+        arrived = {}
+        for g in range(r):
+            for db in range(1, r):
+                arrived[(g + db) % r, db] = shift(partial[g][2], db, 0)
+        for g in list(range(1, r)) + [0]:
+            acc, stat, _ = partial[g]
+            received = [arrived[g, db] for db in range(1, r)]
+            sources = blocks if g == 0 else crosses[(g - 1) * hs : g * hs]
+            p_shape = (per, width) if aligned else (hs, rows, hd)
             combine = pl.pallas_call(
-                functools.partial(combine_kernel, (hs, r, rows, tl, aligned, res_at, g * count, count)),
+                functools.partial(combine_kernel, (hs, r, rows, tl, aligned, res_at if g == 0 else rows)),
                 out_shape=jax.ShapeDtypeStruct(p_shape, BF),
-                in_specs=[SMEM] + [VMEM] * (3 + r - 1 + n),
+                in_specs=[SMEM] + [VMEM] * (3 + r - 1 + hs),
                 out_specs=VMEM,
-                scratch_shapes=[pltpu.VMEM((nq, hd), BF)],
-                compiler_params=params(6 if aligned else 32),
+                scratch_shapes=[pltpu.VMEM((nc, hd), BF)],
+                compiler_params=params(4 if aligned else 32),
             )
-            p = combine(scal, acc, stat, gain2, *received, *blocks, *crosses)
+            p = combine(scal, acc, stat, gain2, *received, *sources)
             if not aligned:
-                p = jnp.moveaxis(p.reshape(count, hp, tl, hd), 1, 2).reshape(per, width)
-            mine.append(p)
+                p = jnp.moveaxis(p.reshape(hs, hp, tl, hd), 1, 2).reshape(per, width)
+            mine[g] = p
         gathered = [[shift(p, 0, d) for p in mine] for d in range(1, hs)]
         (wd,) = prefetch(w_down)
         carry = gate_up((0,), scal, None, mine, gain2, wg, wu, ffp)
@@ -621,22 +614,22 @@
         own, ssq, message = gate_up(tuple(range(1, hs)), scal, carry, flat, gain2, wg, wu, ffp)
         other = lax.ppermute(message, "tensor", [(0, 1), (1, 0)])
 
-        state = own_state(scal, gain2, mine + flat, n, hs, groups, tl)
+        state = own_state(scal, gain2, [mine[0]] + [g[0] for g in gathered], n, hs, tl)
         chunks = 2
         cw = half // chunks
         sums = []
         args = [own, ssq, other]
         for c in range(chunks):
-            pieces = down(c == 0, n, hs, groups, scal, args, wd, c * cw, cw, model)
+            pieces = down(c == 0, n, hs, r, scal, args, wd, c * cw, cw, model)
             if c == 0:
                 args, pieces = [pieces[0]], pieces[1:]
             sums.append((pieces[0], [shift(pieces[d], 0, d) for d in range(1, hs)]))
         outs = []
         for c, (total, got) in enumerate(sums):
-            result, *aways = square_sum(scal, [total] + got, n, hs, r, tl)
+            result, *aways = square_sum([total] + got, r, tl)
             result = state[:, c * cw : (c + 1) * cw] + result
             for db in range(1, r):
-                result = result + shift(aways[db - 1], db, 0).astype(F32)
+                result = result + shift(aways[db - 1], r - db, 0).astype(F32)
             outs.append(result.astype(BF))
         return jnp.concatenate(outs, axis=1).reshape(rl, steps, half)
 

time: 111 us -> 114 us (1.027)
  starting transfers between devices: 28.1 us -> 34.7 us
  waiting for transfers between devices: 41.5 us -> 38.6 us
  Pallas kernels: 39.6 us -> 38.3 us
    ppermute x23, starting transfers between devices: 28 us -> 34.7 us  [shift(): return lax.ppermute(x, 'seq', pairs)]
    ppermute x23, waiting for transfers between devices: 41.5 us -> 38.6 us  [shift(): return lax.ppermute(x, 'seq', pairs)]
    pallas_call x7, Pallas kernels: 10.6 us -> 9.24 us  [the longest x2 7.05 us: body(): partial.append(attend(scal, hbm(row_lengths), *blocks, *extra))]
  transfers between devices with their start and end apart: 24 -> 24, of which waited for: 12 -> 12; matrix products, arithmetic and copies ran while one was open for 0% -> 0% of each run, Pallas kernels for 22% -> 21%
where the time goes in v2:
time: 114 us; the launch traced here: 113 us
  waiting for transfers between devices  38.6 us (34%)
  Pallas kernels  38.3 us (34%)
  starting transfers between devices  34.7 us (30%)
  local copies, waits for them, and re-layouts  1.48 us (1%)
    ppermute x23, waiting for transfers between devices, shift(): return lax.ppermute(x, 'seq', pairs)  38.6 us
    ppermute x23, starting transfers between devices, shift(): return lax.ppermute(x, 'seq', pairs)  34.7 us
    pallas_call x2, Pallas kernels, prefetch(): pl.pallas_call(functools.partial(prefetch_kernel, count, pieces), out_sha...  14.8 us
    pallas_call x2, Pallas kernels, gate_up(): pl.pallas_call(functools.partial(gate_up_kernel, (first, offsets, halves,...  8.1 us
    pallas_call x2, Pallas kernels, body(): partial.append(attend(scal, hbm(row_lengths), *blocks, *extra))  7.05 us
    pallas_call x2, Pallas kernels, down(): pl.pallas_call(functools.partial(down_kernel, (first, n, hs, groups, ffl,...  3.79 us
    pallas_call x1, Pallas kernels, body(): pl.pallas_call(functools.partial(pack_kernel, (hs, n, span, pages, rows,...  2.35 us
  transfers between devices with their start and end apart: 24, of which 12 were waited for; matrix products, arithmetic and copies ran while one was open for 0% of the time, Pallas kernels for 21%

profile of v2, /device:TPU:0, one launch (start us, length us, event | category | flops | bytes accessed | tf_op | source)
XLA Modules:
  0.0 113.4 jit_solution(15265357651990400398)
XLA Ops:
  0.0 2.3 %shard_map.136 = (bf16[1376,128]{1,0:T(8,128)(2,1)S(1)}, bf16[1376,128]{1,0:T(8,128)(2,1)S(1)}, bf16[1376,128]{1,0:T(8,128)(2,1)S(1)}, bf16[1376,128]{1,0:T(8,12...) custom-call(s32[13]{0:T(128)S(1)} %compare_select_fusion.5.scal, ...), custom_call_target="tpu_custom_call" | custom-call | tf_op jit(solution)/shard_map/pallas_call | solution.py:506
  2.4 3.1 %collective-permute-start = (bf16[1376,128]{1,0:T(8,128)(2,1)S(1)}, bf16[1376,128]{1,0:T(8,128)(2,1)S(1)}, u32[]{:S(2)}, u32[]{:S(2)}) collective-permute-start(bf16[1376,128]{1,0:T(8,128)(2,1)S(1)} %get-tuple-element.40), channel_id=1, source_target_pairs={{0,2},{2,0},{4,6},{6,4},{8,10},{10,8},{12,14},{14,12},{1,3},{3,1},... | collective-permute-start | bytes 1056776 | tf_op jit(solution)/shard_map/ppermute | solution.py:497
  5.4 1.6 %collective-permute-start.1 = (bf16[1376,128]{1,0:T(8,128)(2,1)S(1)}, bf16[1376,128]{1,0:T(8,128)(2,1)S(1)}, u32[]{:S(2)}, u32[]{:S(2)}) collective-permute-start(bf16[1376,128]{1,0:T(8,128)(2,1)S(1)} %get-tuple-element.41), channel_id=1, source_target_pairs={{0,4},{2,6},{4,0},{6,2},{8,12},{10,14},{12,8},{14,10},{1,5},{3,7},... | collective-permute-start | bytes 1056776 | tf_op jit(solution)/shard_map/ppermute | solution.py:497
  7.0 6.7 %collective-permute-done.refs_1_.refs_2_ = bf16[1376,128]{1,0:T(8,128)(2,1)S(1)} collective-permute-done((bf16[1376,128]{1,0:T(8,128)(2,1)S(1)}, bf16[1376,128]{1,0:T(8,128)(2,1)S(1)}, u32[]{:S(2)}, u32[]{:S(2)}) %collective-permute-start) | collective-permute-done | bytes 352288 | tf_op jit(solution)/shard_map/ppermute | solution.py:497
  13.7 2.9 %collective-permute-done.1.refs_2_.refs_3_ = bf16[1376,128]{1,0:T(8,128)(2,1)S(1)} collective-permute-done((bf16[1376,128]{1,0:T(8,128)(2,1)S(1)}, bf16[1376,128]{1,0:T(8,128)(2,1)S(1)}, u32[]{:S(2)}, u32[]{:S(2)}) %collective-permute-start.1) | collective-permute-done | bytes 352288 | tf_op jit(solution)/shard_map/ppermute | solution.py:497
  16.5 5.9 %collective-permute-done.2.refs_3_.refs_4_ = bf16[1376,128]{1,0:T(8,128)(2,1)S(1)} collective-permute-done((bf16[1376,128]{1,0:T(8,128)(2,1)S(1)}, bf16[1376,128]{1,0:T(8,128)(2,1)S(1)}, u32[]{:S(2)}, u32[]{:S(2)}) %collective-permute-start.2) | collective-permute-done | bytes 352288 | tf_op jit(solution)/shard_map/ppermute | solution.py:497
  22.5 3.6 %shard_map.137 = (f32[128,512]{1,0:T(8,128)S(1)}, f32[8,512]{1,0:T(8,128)S(1)}, bf16[144,512]{1,0:T(8,128)(2,1)S(1)}) custom-call(s32[13]{0:T(128)S(1)} %compare_select_fusion.5.scal, s32[64]{0:T(128)} %row_len.3, bf16[1376,128]{1,0:T(8,128)(2,1)S(1)} %get-tuple-element.39.refs_0_.refs_1_, bf16[1376,128]{1,0:T(8,128)(2,1)S(1)} %collective-permute-done.refs_1_.refs_2_, ...), custom_call_target="tpu_custom_call" | custom-call | tf_op jit(solution)/shard_map/pallas_call | solution.py:587
  26.1 2.8 %collective-permute-start.11 = (bf16[144,512]{1,0:T(8,128)(2,1)S(1)}, bf16[144,512]{1,0:T(8,128)(2,1)S(1)}, u32[]{:S(2)}, u32[]{:S(2)}) collective-permute-start(bf16[144,512]{1,0:T(8,128)(2,1)S(1)} %get-tuple-element.52), channel_id=1, source_target_pairs={{0,8},{2,10},{4,12},{6,14},{8,0},{10,2},{12,4},{14,6},{1,9},{3,11}... | collective-permute-start | bytes 442376 | tf_op jit(solution)/shard_map/ppermute | solution.py:497
  29.0 3.7 %collective-permute-start.4 = (bf16[256,128]{1,0:T(8,128)(2,1)S(1)}, bf16[256,128]{1,0:T(8,128)(2,1)S(1)}, u32[]{:S(2)}, u32[]{:S(2)}) collective-permute-start(bf16[256,128]{1,0:T(8,128)(2,1)S(1)} %get-tuple-element.46), channel_id=1, source_target_pairs={{0,10},{2,8},{4,14},{6,12},{8,2},{10,0},{12,6},{14,4},{1,11},{3,9}... | collective-permute-start | bytes 196616 | tf_op jit(solution)/shard_map/ppermute | solution.py:497
  32.7 1.3 %collective-permute-start.5 = (bf16[256,128]{1,0:T(8,128)(2,1)S(1)}, bf16[256,128]{1,0:T(8,128)(2,1)S(1)}, u32[]{:S(2)}, u32[]{:S(2)}) collective-permute-start(bf16[256,128]{1,0:T(8,128)(2,1)S(1)} %get-tuple-element.47), channel_id=1, source_target_pairs={{0,12},{2,14},{4,8},{6,10},{8,4},{10,6},{12,0},{14,2},{1,13},{3,15... | collective-permute-start | bytes 196616 | tf_op jit(solution)/shard_map/ppermute | solution.py:497
  34.1 2.4 %collective-permute-start.6 = (bf16[256,128]{1,0:T(8,128)(2,1)S(1)}, bf16[256,128]{1,0:T(8,128)(2,1)S(1)}, u32[]{:S(2)}, u32[]{:S(2)}) collective-permute-start(bf16[256,128]{1,0:T(8,128)(2,1)S(1)} %get-tuple-element.48), channel_id=1, source_target_pairs={{0,14},{2,12},{4,10},{6,8},{8,6},{10,4},{12,2},{14,0},{1,15},{3,13... | collective-permute-start | bytes 196616 | tf_op jit(solution)/shard_map/ppermute | solution.py:497
  36.5 6.4 %collective-permute-done.3.refs_4_.refs_1_ = bf16[256,128]{1,0:T(8,128)(2,1)S(1)} collective-permute-done((bf16[256,128]{1,0:T(8,128)(2,1)S(1)}, bf16[256,128]{1,0:T(8,128)(2,1)S(1)}, u32[]{:S(2)}, u32[]{:S(2)}) %collective-permute-start.3) | collective-permute-done | bytes 65568 | tf_op jit(solution)/shard_map/ppermute | solution.py:497
  42.9 2.4 %collective-permute-done.4.refs_5_.refs_2_ = bf16[256,128]{1,0:T(8,128)(2,1)S(1)} collective-permute-done((bf16[256,128]{1,0:T(8,128)(2,1)S(1)}, bf16[256,128]{1,0:T(8,128)(2,1)S(1)}, u32[]{:S(2)}, u32[]{:S(2)}) %collective-permute-start.4) | collective-permute-done | bytes 65568 | tf_op jit(solution)/shard_map/ppermute | solution.py:497
  45.3 3.5 %shard_map.138 = (f32[128,512]{1,0:T(8,128)S(1)}, f32[8,512]{1,0:T(8,128)S(1)}, bf16[144,512]{1,0:T(8,128)(2,1)S(1)}) custom-call(s32[13]{0:T(128)S(1)} %compare_select_fusion.5.scal, s32[64]{0:T(128)} %row_len.3, bf16[1376,128]{1,0:T(8,128)(2,1)S(1)} %get-tuple-element.39.refs_0_.refs_1_, bf16[1376,128]{1,0:T(8,128)(2,1)S(1)} %collective-permute-done.refs_1_.refs_2_, ...), custom_call_target="tpu_custom_call" | custom-call | tf_op jit(solution)/shard_map/pallas_call | solution.py:587
  48.8 4.4 %collective-permute-start.7 = (bf16[144,512]{1,0:T(8,128)(2,1)S(1)}, bf16[144,512]{1,0:T(8,128)(2,1)S(1)}, u32[]{:S(2)}, u32[]{:S(2)}) collective-permute-start(bf16[144,512]{1,0:T(8,128)(2,1)S(1)} %get-tuple-element.49), channel_id=1, source_target_pairs={{0,8},{2,10},{4,12},{6,14},{8,0},{10,2},{12,4},{14,6},{1,9},{3,11}... | collective-permute-start | bytes 442376 | tf_op jit(solution)/shard_map/ppermute | solution.py:497
  55.1 3.0 %collective-permute-start.14 = (bf16[64,1024]{1,0:T(8,128)(2,1)S(1)}, bf16[64,1024]{1,0:T(8,128)(2,1)S(1)}, u32[]{:S(2)}, u32[]{:S(2)}) collective-permute-start(bf16[64,1024]{1,0:T(8,128)(2,1)S(1)} %shard_map.141.refs_1_), channel_id=1, source_target_pairs={{0,6},{2,4},{4,2},{6,0},{8,14},{10,12},{12,10},{14,8},{1,7},{3,5},... | collective-permute-start | bytes 393224 | tf_op jit(solution)/shard_map/ppermute | solution.py:497
  58.1 1.5 %collective-permute-done.7.refs_0_ = bf16[144,512]{1,0:T(8,128)(2,1)S(1)} collective-permute-done((bf16[144,512]{1,0:T(8,128)(2,1)S(1)}, bf16[144,512]{1,0:T(8,128)(2,1)S(1)}, u32[]{:S(2)}, u32[]{:S(2)}) %collective-permute-start.7) | collective-permute-done | bytes 147488 | tf_op jit(solution)/shard_map/ppermute | solution.py:497
  60.4 1.4 %collective-permute-start.8 = (bf16[64,1024]{1,0:T(8,128)(2,1)S(1)}, bf16[64,1024]{1,0:T(8,128)(2,1)S(1)}, u32[]{:S(2)}, u32[]{:S(2)}) collective-permute-start(bf16[64,1024]{1,0:T(8,128)(2,1)S(1)} %shard_map.139.refs_0_), channel_id=1, source_target_pairs={{0,2},{2,0},{4,6},{6,4},{8,10},{10,8},{12,14},{14,12},{1,3},{3,1},... | collective-permute-start | bytes 393224 | tf_op jit(solution)/shard_map/ppermute | solution.py:497
  61.8 2.1 %collective-permute-start.9 = (bf16[64,1024]{1,0:T(8,128)(2,1)S(1)}, bf16[64,1024]{1,0:T(8,128)(2,1)S(1)}, u32[]{:S(2)}, u32[]{:S(2)}) collective-permute-start(bf16[64,1024]{1,0:T(8,128)(2,1)S(1)} %shard_map.139.refs_0_), channel_id=1, source_target_pairs={{0,4},{2,6},{4,0},{6,2},{8,12},{10,14},{12,8},{14,10},{1,5},{3,7},... | collective-permute-start | bytes 393224 | tf_op jit(solution)/shard_map/ppermute | solution.py:497
  63.9 9.5 %shard_map.142 = (bf16[4096,1792]{1,0:T(8,128)(2,1)S(1)}, bf16[4096,1792]{1,0:T(8,128)(2,1)S(1)}) custom-call(bf16[4096,1792]{1,0:T(8,128)(2,1)} %refs_0_.2, bf16[4096,1792]{1,0:T(8,128)(2,1)} %refs_1_.1), custom_call_target="tpu_custom_call" | custom-call | tf_op jit(solution)/shard_map/pallas_call | solution.py:254
  73.4 2.9 %shard_map.143 = (f32[128,3584]{1,0:T(8,128)S(1)}, f32[128,128]{1,0:T(8,128)S(1)}) custom-call(s32[13]{0:T(128)S(1)} %compare_select_fusion.5.scal, bf16[64,1024]{1,0:T(8,128)(2,1)S(1)} %shard_map.139.refs_0_, bf16[64,1024]{1,0:T(8,128)(2,1)S(1)} %shard_map.141.refs_1_, f32[1,4096]{1,0:T(1,128)S(1)} %bitcast.3, ...), custom_call_target="tpu_custom_call" | custom-call | tf_op jit(solution)/shard_map/pallas_call | solution.py:339
  76.4 5.2 %shard_map.144 = (f32[128,3584]{1,0:T(8,128)S(1)}, f32[128,128]{1,0:T(8,128)S(1)}, bf16[128,3712]{1,0:T(8,128)(2,1)S(1)}) custom-call(s32[13]{0:T(128)S(1)} %compare_select_fusion.5.scal, f32[128,3584]{1,0:T(8,128)S(1)} %get-tuple-element.55.refs_0_, f32[128,128]{1,0:T(8,128)S(1)} %get-tuple-element.56.refs_1_, ...), custom_call_target="tpu_custom_call" | custom-call | tf_op jit(solution)/shard_map/pallas_call | solution.py:339
  81.6 5.3 %shard_map.145.refs_3_.refs_1_ = bf16[1792,4096]{1,0:T(8,128)(2,1)S(1)} custom-call(bf16[1792,4096]{1,0:T(8,128)(2,1)} %refs_0_.3), custom_call_target="tpu_custom_call" | custom-call | tf_op jit(solution)/shard_map/pallas_call | solution.py:254
  86.9 2.1 %shard_map.146 = (bf16[128,1792]{1,0:T(8,128)(2,1)S(1)}, f32[32,2048]{1,0:T(8,128)S(1)}, bf16[32,2048]{1,0:T(8,128)(2,1)S(1)}, bf16[32,2048]{1,0:T(8,128)(2,1)S(1)}, bf16[32,2048]{1,0:T(8,128)(2,1)S(1)}) custom-call(s32[13]{0:T(128)S(1)} %compare_select_fusion.5.scal, f32[128,3584]{1,0:T(8,128)S(1)} %get-tuple-element.57.refs_0_, ...), custom_call_target="tpu_custom_call" | custom-call | tf_op jit(solution)/shard_map/pallas_call | solution.py:394
  89.0 1.7 %shard_map.148 = (f32[32,2048]{1,0:T(8,128)S(1)}, bf16[32,2048]{1,0:T(8,128)(2,1)S(1)}, bf16[32,2048]{1,0:T(8,128)(2,1)S(1)}, bf16[32,2048]{1,0:T(8,128)(2,1)S(1)}) custom-call(s32[13]{0:T(128)S(1)} %compare_select_fusion.5.scal, bf16[128,1792]{1,0:T(8,128)(2,1)S(1)} %get-tuple-element.66.refs_0_, bf16[1792,4096]{1,0:T(8,128)(2,1)S(1)} %shard_map.145.refs_3_.refs_1_), custom_call_target="tpu_custom_call" | custom-call | tf_op jit(solution)/shard_map/pallas_call | solution.py:394
  90.7 1.4 %collective-permute-start.20 = (bf16[32,2048]{1,0:T(8,128)(2,1)S(1)}, bf16[32,2048]{1,0:T(8,128)(2,1)S(1)}, u32[]{:S(2)}, u32[]{:S(2)}) collective-permute-start(bf16[32,2048]{1,0:T(8,128)(2,1)S(1)} %get-tuple-element.68), channel_id=1, source_target_pairs={{0,2},{2,0},{4,6},{6,4},{8,10},{10,8},{12,14},{14,12},{1,3},{3,1},... | collective-permute-start | bytes 393224 | tf_op jit(solution)/shard_map/ppermute | solution.py:497
  92.1 2.2 %collective-permute-start.22 = (bf16[32,2048]{1,0:T(8,128)(2,1)S(1)}, bf16[32,2048]{1,0:T(8,128)(2,1)S(1)}, u32[]{:S(2)}, u32[]{:S(2)}) collective-permute-start(bf16[32,2048]{1,0:T(8,128)(2,1)S(1)} %get-tuple-element.70), channel_id=1, source_target_pairs={{0,6},{2,4},{4,2},{6,0},{8,14},{10,12},{12,10},{14,8},{1,7},{3,5},... | collective-permute-start | bytes 393224 | tf_op jit(solution)/shard_map/ppermute | solution.py:497
  94.3 1.3 %collective-permute-start.16 = (bf16[32,2048]{1,0:T(8,128)(2,1)S(1)}, bf16[32,2048]{1,0:T(8,128)(2,1)S(1)}, u32[]{:S(2)}, u32[]{:S(2)}) collective-permute-start(bf16[32,2048]{1,0:T(8,128)(2,1)S(1)} %get-tuple-element.61), channel_id=1, source_target_pairs={{0,2},{2,0},{4,6},{6,4},{8,10},{10,8},{12,14},{14,12},{1,3},{3,1},... | collective-permute-start | bytes 393224 | tf_op jit(solution)/shard_map/ppermute | solution.py:497
  98.5 3.0 %collective-permute-done.22.refs_3_ = bf16[32,2048]{1,0:T(8,128)(2,1)S(1)} collective-permute-done((bf16[32,2048]{1,0:T(8,128)(2,1)S(1)}, bf16[32,2048]{1,0:T(8,128)(2,1)S(1)}, u32[]{:S(2)}, u32[]{:S(2)}) %collective-permute-start.22) | collective-permute-done | bytes 131104 | tf_op jit(solution)/shard_map/ppermute | solution.py:497
  102.8 2.0 %collective-permute-done.17.refs_2_ = bf16[32,2048]{1,0:T(8,128)(2,1)S(1)} collective-permute-done((bf16[32,2048]{1,0:T(8,128)(2,1)S(1)}, bf16[32,2048]{1,0:T(8,128)(2,1)S(1)}, u32[]{:S(2)}, u32[]{:S(2)}) %collective-permute-start.17) | collective-permute-done | bytes 131104 | tf_op jit(solution)/shard_map/ppermute | solution.py:497
  104.9 2.4 %collective-permute-done.18.refs_3_ = bf16[32,2048]{1,0:T(8,128)(2,1)S(1)} collective-permute-done((bf16[32,2048]{1,0:T(8,128)(2,1)S(1)}, bf16[32,2048]{1,0:T(8,128)(2,1)S(1)}, u32[]{:S(2)}, u32[]{:S(2)}) %collective-permute-start.18) | collective-permute-done | bytes 131104 | tf_op jit(solution)/shard_map/ppermute | solution.py:497
  109.0 3.5 %collective-permute-done.19 = bf16[16,2048]{1,0:T(8,128)(2,1)S(1)} collective-permute-done((bf16[16,2048]{1,0:T(8,128)(2,1)S(1)}, bf16[16,2048]{1,0:T(8,128)(2,1)S(1)}, u32[]{:S(2)}, u32[]{:S(2)}) %collective-permute-start.19) | collective-permute-done | bytes 65568 | tf_op jit(solution)/shard_map/ppermute | solution.py:497
  (38 shorter events, 9.9 us)
Async XLA Ops:
  2.4 11.3 %collective-permute-start = (bf16[1376,128]{1,0:T(8,128)(2,1)S(1)}, bf16[1376,128]{1,0:T(8,128)(2,1)S(1)}, u32[]{:S(2)}, u32[]{:S(2)}) collective-permute-start(bf16[1376,128]{1,0:T(8,128)(2,1)S(1)} %get-tuple-element.40), channel_id=1, source_target_pairs={{0,2},{2,0},{4,6},{6,4},{8,10},{10,8},{12,14},{14,12},{1,3},{3,1},... | collective-permute-start | bytes 1056776 | tf_op jit(solution)/shard_map/ppermute | solution.py:497
  5.4 11.1 %collective-permute-start.1 = (bf16[1376,128]{1,0:T(8,128)(2,1)S(1)}, bf16[1376,128]{1,0:T(8,128)(2,1)S(1)}, u32[]{:S(2)}, u32[]{:S(2)}) collective-permute-start(bf16[1376,128]{1,0:T(8,128)(2,1)S(1)} %get-tuple-element.41), channel_id=1, source_target_pairs={{0,4},{2,6},{4,0},{6,2},{8,12},{10,14},{12,8},{14,10},{1,5},{3,7},... | collective-permute-start | bytes 1056776 | tf_op jit(solution)/shard_map/ppermute | solution.py:497
  7.0 15.5 %collective-permute-start.2 = (bf16[1376,128]{1,0:T(8,128)(2,1)S(1)}, bf16[1376,128]{1,0:T(8,128)(2,1)S(1)}, u32[]{:S(2)}, u32[]{:S(2)}) collective-permute-start(bf16[1376,128]{1,0:T(8,128)(2,1)S(1)} %get-tuple-element.42), channel_id=1, source_target_pairs={{0,6},{2,4},{4,2},{6,0},{8,14},{10,12},{12,10},{14,8},{1,7},{3,5},... | collective-permute-start | bytes 1056776 | tf_op jit(solution)/shard_map/ppermute | solution.py:497
  26.1 27.1 %collective-permute-start.11 = (bf16[144,512]{1,0:T(8,128)(2,1)S(1)}, bf16[144,512]{1,0:T(8,128)(2,1)S(1)}, u32[]{:S(2)}, u32[]{:S(2)}) collective-permute-start(bf16[144,512]{1,0:T(8,128)(2,1)S(1)} %get-tuple-element.52), channel_id=1, source_target_pairs={{0,8},{2,10},{4,12},{6,14},{8,0},{10,2},{12,4},{14,6},{1,9},{3,11}... | collective-permute-start | bytes 442376 | tf_op jit(solution)/shard_map/ppermute | solution.py:497
  28.9 14.1 %collective-permute-start.3 = (bf16[256,128]{1,0:T(8,128)(2,1)S(1)}, bf16[256,128]{1,0:T(8,128)(2,1)S(1)}, u32[]{:S(2)}, u32[]{:S(2)}) collective-permute-start(bf16[256,128]{1,0:T(8,128)(2,1)S(1)} %get-tuple-element.45), channel_id=1, source_target_pairs={{0,8},{2,10},{4,12},{6,14},{8,0},{10,2},{12,4},{14,6},{1,9},{3,11}... | collective-permute-start | bytes 196616 | tf_op jit(solution)/shard_map/ppermute | solution.py:497
  29.0 16.2 %collective-permute-start.4 = (bf16[256,128]{1,0:T(8,128)(2,1)S(1)}, bf16[256,128]{1,0:T(8,128)(2,1)S(1)}, u32[]{:S(2)}, u32[]{:S(2)}) collective-permute-start(bf16[256,128]{1,0:T(8,128)(2,1)S(1)} %get-tuple-element.46), channel_id=1, source_target_pairs={{0,10},{2,8},{4,14},{6,12},{8,2},{10,0},{12,6},{14,4},{1,11},{3,9}... | collective-permute-start | bytes 196616 | tf_op jit(solution)/shard_map/ppermute | solution.py:497
  32.7 12.5 %collective-permute-start.5 = (bf16[256,128]{1,0:T(8,128)(2,1)S(1)}, bf16[256,128]{1,0:T(8,128)(2,1)S(1)}, u32[]{:S(2)}, u32[]{:S(2)}) collective-permute-start(bf16[256,128]{1,0:T(8,128)(2,1)S(1)} %get-tuple-element.47), channel_id=1, source_target_pairs={{0,12},{2,14},{4,8},{6,10},{8,4},{10,6},{12,0},{14,2},{1,13},{3,15... | collective-permute-start | bytes 196616 | tf_op jit(solution)/shard_map/ppermute | solution.py:497
  34.1 11.2 %collective-permute-start.6 = (bf16[256,128]{1,0:T(8,128)(2,1)S(1)}, bf16[256,128]{1,0:T(8,128)(2,1)S(1)}, u32[]{:S(2)}, u32[]{:S(2)}) collective-permute-start(bf16[256,128]{1,0:T(8,128)(2,1)S(1)} %get-tuple-element.48), channel_id=1, source_target_pairs={{0,14},{2,12},{4,10},{6,8},{8,6},{10,4},{12,2},{14,0},{1,15},{3,13... | collective-permute-start | bytes 196616 | tf_op jit(solution)/shard_map/ppermute | solution.py:497
  48.8 10.8 %collective-permute-start.7 = (bf16[144,512]{1,0:T(8,128)(2,1)S(1)}, bf16[144,512]{1,0:T(8,128)(2,1)S(1)}, u32[]{:S(2)}, u32[]{:S(2)}) collective-permute-start(bf16[144,512]{1,0:T(8,128)(2,1)S(1)} %get-tuple-element.49), channel_id=1, source_target_pairs={{0,8},{2,10},{4,12},{6,14},{8,0},{10,2},{12,4},{14,6},{1,9},{3,11}... | collective-permute-start | bytes 442376 | tf_op jit(solution)/shard_map/ppermute | solution.py:497
  53.1 0.7 copy-start
  54.6 7.2 %collective-permute-start.12 = (bf16[64,1024]{1,0:T(8,128)(2,1)S(1)}, bf16[64,1024]{1,0:T(8,128)(2,1)S(1)}, u32[]{:S(2)}, u32[]{:S(2)}) collective-permute-start(bf16[64,1024]{1,0:T(8,128)(2,1)S(1)} %shard_map.141.refs_1_), channel_id=1, source_target_pairs={{0,2},{2,0},{4,6},{6,4},{8,10},{10,8},{12,14},{14,12},{1,3},{3,1},... | collective-permute-start | bytes 393224 | tf_op jit(solution)/shard_map/ppermute | solution.py:497
  55.1 21.2 %collective-permute-start.13 = (bf16[64,1024]{1,0:T(8,128)(2,1)S(1)}, bf16[64,1024]{1,0:T(8,128)(2,1)S(1)}, u32[]{:S(2)}, u32[]{:S(2)}) collective-permute-start(bf16[64,1024]{1,0:T(8,128)(2,1)S(1)} %shard_map.141.refs_1_), channel_id=1, source_target_pairs={{0,4},{2,6},{4,0},{6,2},{8,12},{10,14},{12,8},{14,10},{1,5},{3,7},... | collective-permute-start | bytes 393224 | tf_op jit(solution)/shard_map/ppermute | solution.py:497
  55.1 21.2 %collective-permute-start.14 = (bf16[64,1024]{1,0:T(8,128)(2,1)S(1)}, bf16[64,1024]{1,0:T(8,128)(2,1)S(1)}, u32[]{:S(2)}, u32[]{:S(2)}) collective-permute-start(bf16[64,1024]{1,0:T(8,128)(2,1)S(1)} %shard_map.141.refs_1_), channel_id=1, source_target_pairs={{0,6},{2,4},{4,2},{6,0},{8,14},{10,12},{12,10},{14,8},{1,7},{3,5},... | collective-permute-start | bytes 393224 | tf_op jit(solution)/shard_map/ppermute | solution.py:497
  60.3 13.1 %copy-start.1 = (f32[4096]{0:T(1024)S(1)}, f32[4096]{0:T(1024)}, u32[]{:S(2)}) copy-start(f32[4096]{0:T(1024)} %param.24) | copy-start | bytes 49156
  60.3 16.0 %collective-permute-start.10 = (bf16[64,1024]{1,0:T(8,128)(2,1)S(1)}, bf16[64,1024]{1,0:T(8,128)(2,1)S(1)}, u32[]{:S(2)}, u32[]{:S(2)}) collective-permute-start(bf16[64,1024]{1,0:T(8,128)(2,1)S(1)} %shard_map.139.refs_0_), channel_id=1, source_target_pairs={{0,6},{2,4},{4,2},{6,0},{8,14},{10,12},{12,10},{14,8},{1,7},{3,5},... | collective-permute-start | bytes 393224 | tf_op jit(solution)/shard_map/ppermute | solution.py:497
  60.4 15.9 %collective-permute-start.8 = (bf16[64,1024]{1,0:T(8,128)(2,1)S(1)}, bf16[64,1024]{1,0:T(8,128)(2,1)S(1)}, u32[]{:S(2)}, u32[]{:S(2)}) collective-permute-start(bf16[64,1024]{1,0:T(8,128)(2,1)S(1)} %shard_map.139.refs_0_), channel_id=1, source_target_pairs={{0,2},{2,0},{4,6},{6,4},{8,10},{10,8},{12,14},{14,12},{1,3},{3,1},... | collective-permute-start | bytes 393224 | tf_op jit(solution)/shard_map/ppermute | solution.py:497
  61.8 14.5 %collective-permute-start.9 = (bf16[64,1024]{1,0:T(8,128)(2,1)S(1)}, bf16[64,1024]{1,0:T(8,128)(2,1)S(1)}, u32[]{:S(2)}, u32[]{:S(2)}) collective-permute-start(bf16[64,1024]{1,0:T(8,128)(2,1)S(1)} %shard_map.139.refs_0_), channel_id=1, source_target_pairs={{0,4},{2,6},{4,0},{6,2},{8,12},{10,14},{12,8},{14,10},{1,5},{3,7},... | collective-permute-start | bytes 393224 | tf_op jit(solution)/shard_map/ppermute | solution.py:497
  81.6 5.4 %collective-permute-start.15 = (bf16[128,3712]{1,0:T(8,128)(2,1)S(1)}, bf16[128,3712]{1,0:T(8,128)(2,1)S(1)}, u32[]{:S(2)}, u32[]{:S(2)}) collective-permute-start(bf16[128,3712]{1,0:T(8,128)(2,1)S(1)} %get-tuple-element.59), channel_id=1, source_target_pairs={{0,1},{1,0},{2,3},{3,2},{4,5},{5,4},{6,7},{7,6},{8,9},{9,8},{10,11... | collective-permute-start | bytes 2850824 | tf_op jit(solution)/shard_map/ppermute | solution.py:615
  90.7 6.1 %collective-permute-start.20 = (bf16[32,2048]{1,0:T(8,128)(2,1)S(1)}, bf16[32,2048]{1,0:T(8,128)(2,1)S(1)}, u32[]{:S(2)}, u32[]{:S(2)}) collective-permute-start(bf16[32,2048]{1,0:T(8,128)(2,1)S(1)} %get-tuple-element.68), channel_id=1, source_target_pairs={{0,2},{2,0},{4,6},{6,4},{8,10},{10,8},{12,14},{14,12},{1,3},{3,1},... | collective-permute-start | bytes 393224 | tf_op jit(solution)/shard_map/ppermute | solution.py:497
  92.1 6.4 %collective-permute-start.21 = (bf16[32,2048]{1,0:T(8,128)(2,1)S(1)}, bf16[32,2048]{1,0:T(8,128)(2,1)S(1)}, u32[]{:S(2)}, u32[]{:S(2)}) collective-permute-start(bf16[32,2048]{1,0:T(8,128)(2,1)S(1)} %get-tuple-element.69), channel_id=1, source_target_pairs={{0,4},{2,6},{4,0},{6,2},{8,12},{10,14},{12,8},{14,10},{1,5},{3,7},... | collective-permute-start | bytes 393224 | tf_op jit(solution)/shard_map/ppermute | solution.py:497
  92.1 9.4 %collective-permute-start.22 = (bf16[32,2048]{1,0:T(8,128)(2,1)S(1)}, bf16[32,2048]{1,0:T(8,128)(2,1)S(1)}, u32[]{:S(2)}, u32[]{:S(2)}) collective-permute-start(bf16[32,2048]{1,0:T(8,128)(2,1)S(1)} %get-tuple-element.70), channel_id=1, source_target_pairs={{0,6},{2,4},{4,2},{6,0},{8,14},{10,12},{12,10},{14,8},{1,7},{3,5},... | collective-permute-start | bytes 393224 | tf_op jit(solution)/shard_map/ppermute | solution.py:497
  94.3 8.5 %collective-permute-start.16 = (bf16[32,2048]{1,0:T(8,128)(2,1)S(1)}, bf16[32,2048]{1,0:T(8,128)(2,1)S(1)}, u32[]{:S(2)}, u32[]{:S(2)}) collective-permute-start(bf16[32,2048]{1,0:T(8,128)(2,1)S(1)} %get-tuple-element.61), channel_id=1, source_target_pairs={{0,2},{2,0},{4,6},{6,4},{8,10},{10,8},{12,14},{14,12},{1,3},{3,1},... | collective-permute-start | bytes 393224 | tf_op jit(solution)/shard_map/ppermute | solution.py:497
  95.6 9.2 %collective-permute-start.17 = (bf16[32,2048]{1,0:T(8,128)(2,1)S(1)}, bf16[32,2048]{1,0:T(8,128)(2,1)S(1)}, u32[]{:S(2)}, u32[]{:S(2)}) collective-permute-start(bf16[32,2048]{1,0:T(8,128)(2,1)S(1)} %get-tuple-element.62), channel_id=1, source_target_pairs={{0,4},{2,6},{4,0},{6,2},{8,12},{10,14},{12,8},{14,10},{1,5},{3,7},... | collective-permute-start | bytes 393224 | tf_op jit(solution)/shard_map/ppermute | solution.py:497
  96.9 10.4 %collective-permute-start.18 = (bf16[32,2048]{1,0:T(8,128)(2,1)S(1)}, bf16[32,2048]{1,0:T(8,128)(2,1)S(1)}, u32[]{:S(2)}, u32[]{:S(2)}) collective-permute-start(bf16[32,2048]{1,0:T(8,128)(2,1)S(1)} %get-tuple-element.63), channel_id=1, source_target_pairs={{0,6},{2,4},{4,2},{6,0},{8,14},{10,12},{12,10},{14,8},{1,7},{3,5},... | collective-permute-start | bytes 393224 | tf_op jit(solution)/shard_map/ppermute | solution.py:497
  101.6 7.5 %collective-permute-start.23 = (bf16[16,2048]{1,0:T(8,128)(2,1)S(1)}, bf16[16,2048]{1,0:T(8,128)(2,1)S(1)}, u32[]{:S(2)}, u32[]{:S(2)}) collective-permute-start(bf16[16,2048]{1,0:T(8,128)(2,1)S(1)} %get-tuple-element.72), channel_id=1, source_target_pairs={{0,8},{2,10},{4,12},{6,14},{8,0},{10,2},{12,4},{14,6},{1,9},{3,11}... | collective-permute-start | bytes 196616 | tf_op jit(solution)/shard_map/ppermute | solution.py:497
  107.3 5.2 %collective-permute-start.19 = (bf16[16,2048]{1,0:T(8,128)(2,1)S(1)}, bf16[16,2048]{1,0:T(8,128)(2,1)S(1)}, u32[]{:S(2)}, u32[]{:S(2)}) collective-permute-start(bf16[16,2048]{1,0:T(8,128)(2,1)S(1)} %get-tuple-element.65), channel_id=1, source_target_pairs={{0,8},{2,10},{4,12},{6,14},{8,0},{10,2},{12,4},{14,6},{1,9},{3,11}... | collective-permute-start | bytes 196616 | tf_op jit(solution)/shard_map/ppermute | solution.py:497
